TPU v7x, 32 devices: a whole 2x2x4 slice. The times are simulated.
32 devices in a mesh: dp: 16 (over z, y, core), tensor: 2 (over x).
Axes of the slice: x: 2, y: 2, z: 4, core: 2. Of those that a mesh axis runs over, the one named last changes fastest.
Arguments:
- tokens_in: bfloat16 [2, 4096, 768], P(None, ('dp', 'tensor')), may hold values from -6 to 6
- positions: int32 [3, 2, 4096], P(None, None, ('dp', 'tensor')), may hold values from 0 to 15
- segment_ids: int32 [2, 16, 256], P(None, 'dp'), may hold values from 0 to 2, never falling along the last dimension, each value on 1 to 128 neighbouring positions
- owners: int32 [10368, 1], replicated, may hold values from 0 to 15; in each aligned block of 10368 rows (0 to 10367, 10368 to 20735, ...) at most 1296 rows name the same one
- master: float32 [20736, 1024], P('dp', 'tensor'), may hold values from -0.21875 to 0.21875
- first_moment: float32 [20736, 1024], P('dp', 'tensor'), may hold values from -112 to 112
- second_moment: float32 [20736, 1024], P('dp', 'tensor'), may hold values from 81.92 to 1638.4
- norm_gains: float32 [2, 1280], replicated, may hold values from 0.5 to 1.5
- norm_biases: float32 [2, 1280], replicated, may hold values from -4 to 4
- norm_first: float32 [4, 1280], replicated, may hold values from -256 to 256
- norm_second: float32 [4, 1280], replicated, may hold values from 2048 to 8192
- cotangent: float32 [2, 4096, 512], P(None, ('dp', 'tensor')), may hold values from -6 to 6
Outputs:
- decoded: float32 [2, 4096, 512], P(None, ('dp', 'tensor'))
- tokens_grad: float32 [2, 4096, 768], P(None, ('dp', 'tensor'))
- new_master: float32 [20736, 1024], P('dp', 'tensor')
- new_first: float32 [20736, 1024], P('dp', 'tensor')
- new_second: float32 [20736, 1024], P('dp', 'tensor')
- new_norms: float32 [4, 1280], replicated
- new_norm_first: float32 [4, 1280], replicated
- new_norm_second: float32 [4, 1280], replicated
Inputs may be any that keep to these rules, and one draw needn't show every extreme that they name: `owners`: every dp index owns at most 1296 blocks, and some index owns exactly 1296. `segment_ids`: along each sequence the tile ids never fall; each tile has 1 to 128 tokens, and some tile has exactly 128.
All inputs are finite; a program needn't handle non-finite values.
Results may differ from a plain program's by a relative error of at most 0.024.
Values may be sent and summed in bfloat16 or wider, within the bound.
A program may use at most 192 MiB of HBM per device.

v0:
```python
from functools import partial

import jax
import jax.numpy as jnp
import ml_dtypes
import numpy as np
from jax import lax
from jax.experimental import pallas as pl
from jax.experimental.pallas import tpu as pltpu
from jax.sharding import PartitionSpec as P

DE = 768
HE = 12
HDE = 64
FFE = 3072
DD = 512
HD = 16
HDD = 32
FFD = 2048
STEP = 10


NORM_EPS = 1e-06
BETA_ONE = 0.5
BETA_TWO = 0.5
LEARN_RATE = 0.03
NORM_RATE = 0.3
WEIGHT_DECAY = 0.05
ADAM_EPS = 1e-08
MASK_FILL = -1000000000.0


def sincos_part(coordinate, part_width):
    halfway = part_width // 2
    frequency = 1.0 / 10000.0 ** (jnp.arange(halfway, dtype=jnp.float32) / halfway)
    angles = coordinate.astype(jnp.float32)[:, None] * frequency[None, :]
    return jnp.concatenate([jnp.sin(angles), jnp.cos(angles)], axis=1)


def sincos_embed(positions, model_width):
    side_width = model_width // 16 * 6
    first_width = model_width - 2 * side_width
    return jnp.concatenate(
        [
            sincos_part(positions[0], first_width),
            sincos_part(positions[1], side_width),
            sincos_part(positions[2], side_width),
        ],
        axis=1,
    )


def slot_table(owners, devices, capacity):
    owner_ids = owners[:, 0]
    onehot = (owner_ids[:, None] == jnp.arange(devices, dtype=jnp.int32)[None, :]).astype(jnp.int32)
    before = jnp.cumsum(onehot, axis=0) - onehot
    owner_rank = jnp.sum(before * onehot, axis=1)
    return owner_ids * capacity + owner_rank


def weight_shapes(tensor_count):
    enc_heads = HE // tensor_count
    dec_heads = HD // tensor_count
    return [
        (DE, 3 * enc_heads * HDE),
        (enc_heads * HDE, DE),
        (DE, FFE // tensor_count),
        (FFE // tensor_count, DE),
        (DE, DD // tensor_count),
        (DD, 3 * dec_heads * HDD),
        (dec_heads * HDD, DD),
        (DD, FFD // tensor_count),
        (FFD // tensor_count, DD),
    ]


def split_flat(flat_vector, shapes):
    pieces = []
    offset = 0
    for matrix_shape in shapes:
        length = matrix_shape[0] * matrix_shape[1]
        pieces.append(flat_vector[offset : offset + length].reshape(matrix_shape))
        offset += length
    return pieces


def adamw(weights, gradient, moment_one, moment_two, decay_rate, step_rate):
    one_new = BETA_ONE * moment_one + (1.0 - BETA_ONE) * gradient
    two_new = BETA_TWO * moment_two + (1.0 - BETA_TWO) * gradient * gradient
    one_hat = one_new / (1.0 - BETA_ONE**STEP)
    two_hat = two_new / (1.0 - BETA_TWO**STEP)
    weights_new = weights - step_rate * (
        one_hat / (jnp.sqrt(two_hat) + ADAM_EPS) + decay_rate * weights
    )
    return (weights_new, one_new, two_new)


def norm_forward(values, gain_row, bias_row):
    center = values - jnp.mean(values, axis=-1, keepdims=True)
    spread = jnp.mean(center * center, axis=-1, keepdims=True)
    inverse = lax.rsqrt(spread + NORM_EPS)
    normed = center * inverse
    return (normed * gain_row + bias_row, (normed, inverse))


def norm_backward(upstream, stored, gain_row):
    normed, inverse = stored
    scaled = upstream * gain_row
    mean_one = jnp.mean(scaled, axis=-1, keepdims=True)
    mean_two = jnp.mean(scaled * normed, axis=-1, keepdims=True)
    return (
        inverse * (scaled - mean_one - normed * mean_two),
        jnp.sum(upstream * normed, axis=0),
        jnp.sum(upstream, axis=0),
    )


def inner_rows(left_side, right_side):
    return lax.dot_general(
        left_side, right_side, (((0,), (0,)), ((), ())), preferred_element_type=jnp.float32
    )


def times_transpose(left_side, right_side):
    return lax.dot_general(
        left_side, right_side, (((1,), (1,)), ((), ())), preferred_element_type=jnp.float32
    )


def gather_rows(values):
    return lax.all_gather(values, "tensor", axis=0, tiled=True)


def gather_grads(values):
    return lax.all_gather(values, "tensor", axis=0, tiled=True)


def branch_rows(values, weight):
    return lax.psum_scatter(
        jnp.dot(values, weight, preferred_element_type=jnp.float32).astype(jnp.bfloat16),
        "tensor",
        scatter_dimension=0,
        tiled=True,
    ).astype(jnp.float32)


def input_rows(values, weight):
    return lax.psum_scatter(
        times_transpose(values, weight).astype(jnp.bfloat16),
        "tensor",
        scatter_dimension=0,
        tiled=True,
    ).astype(jnp.float32)


def block_scores(queries, key_rows, mask_bias, block_start, block_rows, head_size):
    scores = jnp.einsum(
        "qhd,khd->hqk", queries, key_rows, preferred_element_type=jnp.float32
    ) * head_size ** (-0.5)
    return scores + mask_bias[None, block_start : block_start + block_rows]


def attention_forward(gathered, w_qkv, head_count, head_size, mask_bias):
    length = gathered.shape[0]
    projected = jnp.dot(gathered, w_qkv, preferred_element_type=jnp.float32).astype(jnp.bfloat16)
    projected = projected.reshape(length, 3, head_count, head_size)
    queries = projected[:, 0]
    key_rows = projected[:, 1]
    value_rows = projected[:, 2]
    block_rows = min(512, length)
    scores = block_scores(queries, key_rows, mask_bias, 0, block_rows, head_size)
    row_peak = jnp.max(scores, axis=-1, keepdims=True)
    row_total = row_peak + jnp.log(jnp.sum(jnp.exp(scores - row_peak), axis=-1, keepdims=True))
    weights = jnp.exp(scores - row_total).astype(jnp.bfloat16)
    outputs = jnp.einsum("hqk,khd->qhd", weights, value_rows, preferred_element_type=jnp.float32)
    totals = [row_total]
    attended = outputs.astype(jnp.bfloat16).reshape(length, head_count * head_size)
    return (attended, (queries, key_rows, value_rows, totals))


def attention_backward(upstream, w_out, attended, stored, head_count, head_size, mask_bias):
    queries, key_rows, value_rows, totals = stored
    length = upstream.shape[0]
    score_scale = head_size ** (-0.5)
    grad_out = inner_rows(attended, upstream)
    attended_grad = (
        times_transpose(upstream, w_out).astype(jnp.bfloat16).reshape(length, head_count, head_size)
    )
    block_rows = min(512, length)
    key_grads = jnp.zeros((length, head_count, head_size), jnp.float32)
    value_grads = jnp.zeros((length, head_count, head_size), jnp.float32)
    query_grads = []
    for number, block_start in enumerate(range(0, length, block_rows)):
        scores = block_scores(queries, key_rows, mask_bias, block_start, block_rows, head_size)
        weights = jnp.exp(scores - totals[number])
        value_grads = jnp.einsum(
            "hqk,qhd->khd",
            weights.astype(jnp.bfloat16),
            attended_grad,
            preferred_element_type=jnp.float32,
        )
        weight_grads = jnp.einsum(
            "qhd,khd->hqk", attended_grad, value_rows, preferred_element_type=jnp.float32
        )
        score_grads = (
            weights * (weight_grads - jnp.sum(weights * weight_grads, axis=-1, keepdims=True))
        ).astype(jnp.bfloat16)
        query_grads.append(
            jnp.einsum("hqk,khd->qhd", score_grads, key_rows, preferred_element_type=jnp.float32)
            * score_scale
        )
        key_grads = (
            jnp.einsum("hqk,qhd->khd", score_grads, queries, preferred_element_type=jnp.float32)
            * score_scale
        )
    projected_grad = jnp.stack([query_grads[0], key_grads, value_grads], axis=1)
    return (
        projected_grad.astype(jnp.bfloat16).reshape(length, 3 * head_count * head_size),
        grad_out,
    )


def block_forward(residual, matrices, gain_rows, bias_rows, head_count, head_size, mask_bias):
    w_qkv, w_out, w_in, w_down = matrices
    normed, norm_one = norm_forward(residual, gain_rows[0], bias_rows[0])
    gathered = gather_rows(normed.astype(jnp.bfloat16))
    attended, stored = attention_forward(gathered, w_qkv, head_count, head_size, mask_bias)
    middle = residual + branch_rows(attended, w_out)
    normed_two, norm_two = norm_forward(middle, gain_rows[1], bias_rows[1])
    gathered_two = gather_rows(normed_two.astype(jnp.bfloat16))
    hidden = jnp.dot(gathered_two, w_in, preferred_element_type=jnp.float32)
    active = jax.nn.gelu(hidden, approximate=False).astype(jnp.bfloat16)
    result = middle + branch_rows(active, w_down)
    return (result, (gathered, norm_one, attended, stored, gathered_two, norm_two, hidden, active))


def block_backward(upstream, matrices, gain_rows, saved_values, head_count, head_size, mask_bias):
    w_qkv, w_out, w_in, w_down = matrices
    gathered, norm_one, attended, stored, gathered_two, norm_two, hidden, active = saved_values
    down_full = gather_grads(upstream.astype(jnp.bfloat16))
    grad_down = inner_rows(active, down_full)
    active_grad = times_transpose(down_full, w_down)
    gelu_pull = jax.vjp(partial(jax.nn.gelu, approximate=False), hidden)[1]
    hidden_grad = gelu_pull(active_grad)[0].astype(jnp.bfloat16)
    grad_in = inner_rows(gathered_two, hidden_grad)
    normed_two_grad = input_rows(hidden_grad, w_in)
    middle_grad, gain_two, bias_two = norm_backward(normed_two_grad, norm_two, gain_rows[1])
    middle_grad = upstream + middle_grad
    middle_full = gather_grads(middle_grad.astype(jnp.bfloat16))
    projected_grad, grad_out = attention_backward(
        middle_full, w_out, attended, stored, head_count, head_size, mask_bias
    )
    grad_qkv = inner_rows(gathered, projected_grad)
    normed_grad = input_rows(projected_grad, w_qkv)
    input_grad, gain_one, bias_one = norm_backward(normed_grad, norm_one, gain_rows[0])
    return (
        middle_grad + input_grad,
        [grad_qkv, grad_out, grad_in, grad_down],
        (gain_one, gain_two, bias_one, bias_two),
    )


def embed_forward(residual, w_embed):
    residual_low = gather_rows(residual.astype(jnp.bfloat16))
    columns = jnp.dot(residual_low, w_embed, preferred_element_type=jnp.float32).astype(
        jnp.bfloat16
    )
    own_columns = lax.all_to_all(columns, "tensor", split_axis=0, concat_axis=1, tiled=True)
    return (own_columns.astype(jnp.float32), residual_low)


def embed_backward(upstream, residual_low, w_embed):
    columns = lax.all_to_all(
        upstream.astype(jnp.bfloat16), "tensor", split_axis=1, concat_axis=0, tiled=True
    )
    grad_embed = inner_rows(residual_low, columns)
    return (input_rows(columns, w_embed), grad_embed)


def slot_builder(gradients, unit_of_slot, unit_width):
    flat_units = jnp.concatenate([gradient.reshape(-1) for gradient in gradients]).reshape(
        -1, unit_width
    )
    unit_total = flat_units.shape[0]
    source = jnp.take(flat_units, jnp.clip(unit_of_slot, 0, unit_total - 1), axis=0)
    return jnp.where((unit_of_slot >= 0)[:, None], source, 0.0)


def per_device(
    tokens_in,
    positions,
    segment_ids,
    owners,
    master,
    first_moment,
    second_moment,
    norm_gains,
    norm_biases,
    norm_first,
    norm_second,
    cotangent,
):
    devices = lax.axis_size("dp")
    tensor_count = lax.axis_size("tensor")
    capacity = master.shape[0]
    unit_width = master.shape[1]
    unit_count = owners.shape[0]
    slot_index = slot_table(owners, devices, capacity)
    unit_of_slot = (
        jnp.full((devices * capacity,), -1, jnp.int32)
        .at[slot_index]
        .set(jnp.arange(unit_count, dtype=jnp.int32))
    )
    targets = unit_of_slot
    targets = jnp.where(targets < 0, unit_count, targets)
    placed = (
        jnp.zeros((unit_count, unit_width), jnp.bfloat16)
        .at[targets]
        .set(lax.all_gather(master.astype(jnp.bfloat16), "dp", axis=0, tiled=True), mode="drop")
    )
    shapes = weight_shapes(tensor_count)
    matrices = split_flat(placed.reshape(-1), shapes)
    encoder = matrices[0:4]
    w_embed = matrices[4]
    decoder = matrices[5:9]
    enc_heads = HE // tensor_count
    dec_heads = HD // tensor_count
    micro_count = tokens_in.shape[0]
    grad_sums = [jnp.zeros(matrix_shape, jnp.float32) for matrix_shape in shapes]
    norm_sums = jnp.zeros((4, DE + DD), jnp.float32)
    decoded_rows = []
    token_grads = []
    for micro_step in range(micro_count):
        tile_ids = segment_ids[micro_step, 0]
        mask_bias = jnp.where(tile_ids[:, None] == tile_ids[None, :], 0.0, MASK_FILL).astype(
            jnp.float32
        )
        position_now = positions[:, micro_step]
        residual = tokens_in[micro_step].astype(jnp.float32) + sincos_embed(position_now, DE)
        residual, enc_saved = block_forward(
            residual, encoder, norm_gains[:, :DE], norm_biases[:, :DE], enc_heads, HDE, mask_bias
        )
        residual, embed_low = embed_forward(residual, w_embed)
        residual = residual + sincos_embed(position_now, DD)
        residual, dec_saved = block_forward(
            residual, decoder, norm_gains[:, DE:], norm_biases[:, DE:], dec_heads, HDD, mask_bias
        )
        decoded_rows.append(residual)
        upstream, dec_grads, dec_norm = block_backward(
            cotangent[micro_step], decoder, norm_gains[:, DE:], dec_saved, dec_heads, HDD, mask_bias
        )
        upstream, grad_embed = embed_backward(upstream, embed_low, w_embed)
        upstream, enc_grads, enc_norm = block_backward(
            upstream, encoder, norm_gains[:, :DE], enc_saved, enc_heads, HDE, mask_bias
        )
        token_grads.append(upstream)
        step_grads = enc_grads + [grad_embed] + dec_grads
        step_norm = jnp.concatenate([jnp.stack(enc_norm), jnp.stack(dec_norm)], axis=1)
        grad_sums = [total_grad + new_grad for total_grad, new_grad in zip(grad_sums, step_grads)]
        norm_sums = norm_sums + step_norm
    reduced = lax.psum_scatter(
        slot_builder(grad_sums, unit_of_slot, unit_width), "dp", scatter_dimension=0, tiled=True
    )
    norm_total = lax.psum(norm_sums, ("dp", "tensor"))
    new_master, new_first, new_second = adamw(
        master, reduced, first_moment, second_moment, WEIGHT_DECAY, LEARN_RATE
    )
    norm_params = jnp.concatenate([norm_gains, norm_biases], axis=0)
    new_norms, norm_one_new, norm_two_new = adamw(
        norm_params, norm_total, norm_first, norm_second, 0.0, NORM_RATE
    )
    return (
        jnp.stack(decoded_rows),
        jnp.stack(token_grads),
        new_master,
        new_first,
        new_second,
        new_norms,
        norm_one_new,
        norm_two_new,
    )


MESH = pl.DeviceIdType.MESH
ALL = slice(None)


class Place:
    def __init__(self):
        self.d = lax.axis_index("dp")
        self.x = lax.axis_index("tensor")
        self.z = self.d // 4
        self.y = (self.d // 2) % 2
        self.c = self.d % 2
        self.ids = {
            "c": (self.d + 1 - 2 * self.c, self.x),
            "y": (self.d + 2 - 4 * self.y, self.x),
            "x": (self.d, 1 - self.x),
            "z+": (self.d + 4, self.x),
            "z-": (self.d - 4, self.x),
        }

    def greet(self, kinds):
        bar = pltpu.get_barrier_semaphore()
        for k in kinds:
            pl.semaphore_signal(bar, inc=1, device_id=self.ids[k], device_id_type=MESH)

        @pl.when(self.z < 3)
        def _():
            pl.semaphore_signal(bar, inc=1, device_id=self.ids["z+"], device_id_type=MESH)

        @pl.when(self.z > 0)
        def _():
            pl.semaphore_signal(bar, inc=1, device_id=self.ids["z-"], device_id_type=MESH)

        inner = jnp.where(jnp.logical_and(self.z > 0, self.z < 3), 1, 0)
        pl.semaphore_wait(bar, len(kinds) + 1 + inner)

    def there(self, disp):
        dz = disp[0]
        if dz == 0:
            return None
        return self.z + dz <= 3 if dz > 0 else self.z + dz >= 0

    def at(self, disp):
        dz, fy, fx = disp
        return (1 - self.x if fx else self.x, self.z + dz, 1 - self.y if fy else self.y)


def when(cond, f):
    if cond is None:
        f()
    else:
        pl.when(cond)(f)


def both(a, b):
    if a is None:
        return b
    if b is None:
        return a
    return jnp.logical_and(a, b)


def spread(order):
    out = {}
    todo = [((0, 0, 0), -1, 0)]
    while todo:
        (dz, fy, fx), last, way = todo.pop(0)
        nxt = []
        for i, a in enumerate(order):
            if i < last:
                continue
            if a == "z":
                for s in (1, -1):
                    if i == last and s != way:
                        continue
                    n = (dz - s, fy, fx)
                    if abs(n[0]) <= 3:
                        nxt.append((n, "z+" if s > 0 else "z-", i, s))
            elif i > last:
                n = (dz, 1, fx) if a == "y" else (dz, fy, 1)
                nxt.append((n, a, i, 0))
        out[(dz, fy, fx)] = [(n, w) for n, w, _, _ in nxt]
        todo += [(n, i, s) for n, _, i, s in nxt]
    return out


def hops(d):
    return abs(d[0]) + d[1] + d[2]


BACK = {"z+": "z-", "z-": "z+", "x": "x", "y": "y"}


def add_rows(acc, got, step=80):
    n = acc.shape[0]
    while n % step:
        step -= 16

    def body(i, _):
        r = pl.ds(pl.multiple_of(i * step, step), step)
        acc[r, :] = acc[r, :] + got[r, :]
        return 0

    lax.fori_loop(0, n // step, body, 0)


SHARD_UNITS = 656
PANEL = 128
GROUPS = ((0, 1), (2,), (3,), (4, 5, 6), (7, 8))

PLAN_OUT = (
    ("zy", "zy", "yz", "yz", "yz"),
    ("zxy", "yzx", "zyx", "yzx", "xzy"),
    (
        128, 129, 0, 4, 131, 130, 132, 8, 134, 64, 135, 133, 1, 9, 2, 68, 69, 5, 138, 137, 73, 256, 6, 136, 3, 192,
        65, 140, 141, 66, 139, 7, 72, 10, 142, 143, 70, 12, 13, 67, 11, 147, 146, 144, 76, 71, 148, 74, 154, 14, 15,
        75, 77, 16, 193, 257, 162, 258, 19, 78, 194, 79, 320, 259, 168, 260, 196, 26, 197, 261, 20, 156, 80, 83, 82,
        262, 265, 198, 170, 155, 27, 145, 17, 151, 32, 84, 264, 86, 34, 200, 24, 157, 163, 266, 22, 90, 195, 28, 89,
        160, 40, 29, 268, 202, 36, 201, 152, 85, 88, 263, 91, 21, 93, 269, 97, 199, 267, 92, 35, 33, 25, 104, 205, 81,
        204, 203, 39, 270, 271, 167, 150, 206, 207, 23, 272, 31, 273, 101, 276, 37, 98, 210, 41, 100, 38, 42, 275,
        278, 103, 18, 211, 161, 96, 149, 165, 30, 95, 164, 280, 208, 277, 321, 215, 322, 102, 282, 153, 212, 323, 290,
        283, 94, 217, 106, 169, 279, 285, 209, 324, 87, 105, 158, 218, 216, 288, 289, 166, 99, 214, 159, 325, 225,
        284, 219, 326, 226, 220, 292, 327, 227, 221, 291, 224, 213, 294, 295, 328, 230, 296, 228, 293, 281, 274, 232,
        287, 223, 286, 329, 231, 222, 298, 297, 330, 233, 229, 234,
    ),
)
PLAN_BACK = (
    ("zxy", "yzx", "zyx", "yzx", "xzy"),
    ("zy", "zy", "zy", "yz", "yz"),
    (
        256, 257, 258, 262, 261, 269, 64, 259, 67, 260, 65, 69, 263, 66, 78, 264, 271, 278, 276, 77, 270, 268, 267,
        71, 70, 275, 282, 85, 72, 266, 76, 265, 192, 82, 68, 199, 277, 73, 0, 84, 274, 74, 272, 5, 273, 80, 75, 279,
        6, 79, 13, 128, 204, 1, 281, 2, 12, 89, 283, 280, 11, 141, 129, 19, 8, 83, 4, 195, 86, 193, 87, 3, 134, 15, 7,
        81, 284, 285, 133, 88, 91, 14, 10, 197, 194, 90, 22, 196, 132, 286, 131, 201, 288, 287, 130, 16, 18, 21, 198,
        9, 92, 20, 205, 93, 291, 202, 200, 290, 136, 289, 143, 292, 26, 140, 208, 150, 206, 17, 94, 23, 135, 25, 212,
        213, 294, 95, 142, 203, 96, 24, 138, 148, 139, 207, 137, 211, 27, 214, 210, 100, 97, 295, 144, 215, 149, 104,
        146, 209, 147, 28, 29, 151, 218, 219, 217, 145, 154, 32, 101, 153, 106, 30, 216, 36, 155, 152, 296, 33, 220,
        105, 221, 293, 98, 156, 40, 157, 224, 31, 103, 298, 222, 160, 158, 223, 164, 102, 99, 228, 37, 161, 227, 165,
        41, 225, 168, 159, 226, 35, 42, 34, 229, 163, 297, 39, 231, 230, 232, 162, 167, 170, 234, 38, 166, 169, 233,
    ),
)


def layout(shapes, shards):
    table = []
    unit_at, row_at, flat_at = 0, 0, 0
    starts = [g[0] for g in GROUPS]
    for i, (rows, cols) in enumerate(shapes):
        if i in starts:
            unit_at = -(-unit_at // 16) * 16
        rb, panels = rows // shards, cols // PANEL
        units = rb * cols // 512
        padded = -(-rb // 16) * 16
        table.append((rb, panels, units, unit_at, row_at, padded, flat_at))
        unit_at += units
        row_at += padded * panels
        flat_at += units * shards
    return table, unit_at, row_at


def unit_places(units, table, shards):
    place = jnp.zeros_like(units)
    for _, _, n, first, _, _, lo in table:
        v = units - lo
        here = (v // n) * SHARD_UNITS + first + v % n
        place = jnp.where(v >= 0, here, place)
    return place


def own_units(owners, mine, capacity):
    count = owners.shape[0] // 128
    hit = (owners[:, 0] == mine).reshape(count, 128)
    lane = jnp.arange(128)
    tri = (lane[:, None] <= lane[None, :]).astype(jnp.bfloat16)
    within = jnp.dot(hit.astype(jnp.bfloat16), tri, preferred_element_type=jnp.float32)
    totals = within[:, 127].astype(jnp.int32)
    upto = jnp.sum(jnp.where(jnp.arange(count)[:, None] >= jnp.arange(count)[None, :], totals[None, :], 0), axis=1)
    slot = jnp.arange(capacity, dtype=jnp.int32)
    block = jnp.sum((upto[None, :] <= slot[:, None]).astype(jnp.int32), axis=1)
    pick = block[:, None] == jnp.arange(count)[None, :]
    before = jnp.sum(jnp.where(pick, (upto - totals)[None, :], 0), axis=1)
    row = jnp.dot(pick.astype(jnp.bfloat16), within.astype(jnp.bfloat16), preferred_element_type=jnp.float32)
    rank = (slot - before).astype(jnp.float32)
    at = jnp.sum((row <= rank[:, None]).astype(jnp.int32), axis=1)
    return block * 128 + at, slot < upto[count - 1]


BY_ROWS = (1, 3, 6, 8)


def position_table():
    cols = []
    for width in (DE, DD):
        side = width // 16 * 6
        parts = (width - 2 * side, side, side)
        tab = np.zeros((48, width), np.float64)
        col = 0
        for i, n in enumerate(parts):
            half = n // 2
            freq = 1.0 / 10000.0 ** (np.arange(half) / half)
            ang = np.arange(16)[:, None] * freq[None, :]
            tab[16 * i:16 * i + 16, col:col + n] = np.concatenate([np.sin(ang), np.cos(ang)], axis=1)
            col += n
        cols.append(tab)
    left = np.concatenate(cols, axis=1).astype(np.float32)
    terms = []
    for _ in range(3):
        terms.append(left.astype(ml_dtypes.bfloat16))
        left = left - terms[-1].astype(np.float32)
    return np.stack(terms)


def dot(a, b):
    return jnp.dot(a, b, preferred_element_type=jnp.float32)


def dot_nt(a, b):
    return lax.dot_general(a, b, (((1,), (1,)), ((), ())), preferred_element_type=jnp.float32)


def dot_tn(a, b):
    return lax.dot_general(a, b, (((0,), (0,)), ((), ())), preferred_element_type=jnp.float32)


def lanes(i, n=128):
    return pl.ds(pl.multiple_of(i * n, n), n)


def ln_parts(x):
    c = x - jnp.mean(x, axis=-1, keepdims=True)
    inv = lax.rsqrt(jnp.mean(c * c, axis=-1, keepdims=True) + NORM_EPS)
    return c * inv, inv


def ln_back(up, m, inv, gain):
    s = up * gain
    a = jnp.mean(s, axis=-1, keepdims=True)
    b = jnp.mean(s * m, axis=-1, keepdims=True)
    return inv * (s - a - m * b), jnp.sum(up * m, axis=0, keepdims=True), jnp.sum(up, axis=0, keepdims=True)


class Block:
    def __init__(self, width, heads, size, hidden, first, table, col):
        self.width, self.heads, self.size, self.hidden, self.col = width, heads, size, hidden, col
        self.q, self.o, self.a, self.b = table[first:first + 4]
        self.part = heads // 2 * size
        self.per = 128 // size


def panel(w, t, mat, g, lo=0, num=16):
    rb, _, _, _, at, padded, _ = mat
    rows = pl.ds(pl.multiple_of(at + g * padded, 16), padded)
    v = w[t, lo:lo + num, rows, :] if isinstance(lo, int) else w[t, pl.ds(lo, num), rows, :]
    if padded > rb:
        v = v.astype(jnp.float32)[:, :rb].reshape(num * rb, 128).astype(jnp.bfloat16)
        return v
    return v.reshape(num * rb, 128)


def pair(w, mat, g):
    return jnp.concatenate([panel(w, 0, mat, g), panel(w, 1, mat, g)], axis=1)


def repeat(count, step, f):
    step = max(k for k in range(1, step + 1) if count % k == 0)

    def turn(i, _):
        for k in range(step):
            f(i * step + k)
        return 0

    if step == count:
        turn(0, 0)
    else:
        lax.fori_loop(0, count // step, turn, 0)


def pull(acc, up, w, mat, step):
    count = mat[1]
    step = max(k for k in range(1, step + 1) if count % k == 0)

    def part(i):
        gs = [i * step + k for k in range(step)]
        d = jnp.concatenate([up[:, lanes(o + g)] for g in gs for o in (0, count)], axis=1)
        return dot_nt(d, jnp.concatenate([pair(w, mat, g) for g in gs], axis=1))

    acc[...] = part(0)

    def turn(i, _):
        acc[...] += part(i)
        return 0

    lax.fori_loop(1, count // step, turn, 0)


def block_fwd(b, x, xo, w, gains, biases, same, n1, proj, p, att, ow, m1, i1, n2, m2, i2, act, slope,
              need, keep):
    cols = slice(b.col, b.col + b.width)
    m, inv = ln_parts(x[...])
    m1[...] = m
    i1[...] = jnp.broadcast_to(inv, i1.shape)
    n1[...] = (m * gains[0:1, cols] + biases[0:1, cols]).astype(jnp.bfloat16)
    keep(0)
    yield
    need(0)
    gq = b.q[1]

    def qkv(g):
        r = dot(n1[...], pair(w, b.q, g)).astype(jnp.bfloat16)
        proj[:, lanes(g)] = r[:, :128]
        proj[:, lanes(gq + g)] = r[:, 128:]

    repeat(gq, 9, qkv)
    yield
    np_ = b.part // 128
    lane = lax.broadcasted_iota(jnp.int32, (256, 128), 1)
    masks = [lane // b.size == i for i in range(b.per)]

    def heads(i, _):
        t, j = i // np_, i % np_
        q = proj[:, lanes(t * gq + j)]
        k = proj[:, lanes(t * gq + np_ + j)]
        v = proj[:, lanes(t * gq + 2 * np_ + j)]
        total = jnp.zeros((256, 128), jnp.float32)
        for h in range(b.per):
            z = dot_nt(jnp.where(masks[h], q, 0), k) * b.size ** (-0.5) + same
            e = jnp.exp(z - jnp.max(z, axis=-1, keepdims=True))
            s = e * (1.0 / jnp.sum(e, axis=-1, keepdims=True))
            p[i * b.per + h] = s
            total = total + dot(s.astype(jnp.bfloat16), jnp.where(masks[h], v, 0))
        att[:, lanes(i)] = total.astype(jnp.bfloat16)
        return 0

    lax.fori_loop(0, np_, heads, 0)
    yield
    lax.fori_loop(np_, 2 * np_, heads, 0)
    keep(1)
    yield
    need(1)
    for t in range(2):
        for g in range(b.width // 128):
            ow[t, :, g * 128:(g + 1) * 128] = panel(w, t, b.o, g)
    x1 = x[...] + dot(att[:, :b.part], ow[0]) + dot(att[:, b.part:], ow[1])
    xo[...] = x1
    m, inv = ln_parts(x1)
    m2[...] = m
    i2[...] = jnp.broadcast_to(inv, i2.shape)
    n2[...] = (m * gains[1:2, cols] + biases[1:2, cols]).astype(jnp.bfloat16)
    keep(2)
    yield
    need(2)
    ga = b.a[1]

    def up(g):
        h = dot(n2[...], pair(w, b.a, g))
        big = 0.5 * (1.0 + lax.erf(h * 0.7071067811865476))
        act_v = (h * big).astype(jnp.bfloat16)
        dens = big + h * (0.3989422804014327 * jnp.exp(-0.5 * h * h))
        act[:, lanes(g)] = act_v[:, :128]
        act[:, lanes(ga + g)] = act_v[:, 128:]
        slope[:, lanes(g)] = dens[:, :128]
        slope[:, lanes(ga + g)] = dens[:, 128:]

    repeat(ga, 12, up)
    keep(3)
    yield
    need(3)
    half = b.hidden // 2

    def down(g):
        w0 = jnp.concatenate([panel(w, 0, b.b, 2 * g), panel(w, 0, b.b, 2 * g + 1)], axis=1)
        w1 = jnp.concatenate([panel(w, 1, b.b, 2 * g), panel(w, 1, b.b, 2 * g + 1)], axis=1)
        xo[:, lanes(g, 256)] += dot(act[:, :half], w0) + dot(act[:, half:], w1)

    repeat(b.width // 256, 1, down)


def block_bwd(b, dr, w, gains, same, n1, proj, p, att, ow, m1, i1, n2, m2, i2, act, slope,
              r, dh, r1, dp_out, acc, da, norm_out, keep):
    cols = slice(b.col, b.col + b.width)
    r[...] = dr[...].astype(jnp.bfloat16)
    keep(3)
    half = b.hidden // 2
    rb = b.b[0]
    gb = b.width // 128
    num = 16

    def hidden(i, _):
        t, lo = i // (16 // num), (i % (16 // num)) * num
        wc = jnp.concatenate([panel(w, t, b.b, g, lo, num) for g in range(gb)], axis=1)
        at = lanes(i, num * rb)
        dh[:, at] = (dot_nt(r[...], wc) * slope[:, at]).astype(jnp.bfloat16)
        return 0

    lax.fori_loop(0, 2 * (16 // num), hidden, 0)
    keep(2)
    ga = b.a[1]
    pull(acc, dh, w, b.a, 12)
    dx, dg, db = ln_back(acc[...], m2[...], i2[:, :1], gains[1:2, cols])
    norm_out[1:2, cols] = dg
    norm_out[3:4, cols] = db
    dx1 = dr[...] + dx
    dr[...] = dx1
    r1[...] = dx1.astype(jnp.bfloat16)
    keep(1)
    for t in range(2):
        da[:, t * b.part:(t + 1) * b.part] = dot_nt(r1[...], ow[t]).astype(jnp.bfloat16)
    gq = b.q[1]
    np_ = b.part // 128
    lane = lax.broadcasted_iota(jnp.int32, (256, 128), 1)
    masks = [lane // b.size == i for i in range(b.per)]
    scale = b.size ** (-0.5)

    def heads(i, _):
        t, j = i // np_, i % np_
        q = proj[:, lanes(t * gq + j)]
        k = proj[:, lanes(t * gq + np_ + j)]
        v = proj[:, lanes(t * gq + 2 * np_ + j)]
        up_ = da[:, lanes(i)]
        dq = jnp.zeros((256, 128), jnp.float32)
        dk = jnp.zeros((256, 128), jnp.float32)
        dv = jnp.zeros((256, 128), jnp.float32)
        for h in range(b.per):
            s = p[i * b.per + h]
            u = jnp.where(masks[h], up_, 0)
            dp = dot_nt(u, v)
            dv = dv + dot_tn(s.astype(jnp.bfloat16), u)
            t1 = s * dp
            dz = (t1 - s * jnp.sum(t1, axis=-1, keepdims=True)).astype(jnp.bfloat16)
            dq = dq + dot(dz, jnp.where(masks[h], k, 0))
            dk = dk + dot_tn(dz, jnp.where(masks[h], q, 0))
        dp_out[:, lanes(t * gq + j)] = (dq * scale).astype(jnp.bfloat16)
        dp_out[:, lanes(t * gq + np_ + j)] = (dk * scale).astype(jnp.bfloat16)
        dp_out[:, lanes(t * gq + 2 * np_ + j)] = dv.astype(jnp.bfloat16)
        return 0

    lax.fori_loop(0, 2 * np_, heads, 0)
    keep(0)
    pull(acc, dp_out, w, b.q, 9)
    dx, dg, db = ln_back(acc[...], m1[...], i1[:, :1], gains[0:1, cols])
    norm_out[0:1, cols] = dg
    norm_out[2:3, cols] = db
    dr[...] = dr[...] + dx


ACTS = (DE, DE, DE, FFE, DE, DD, DD, DD, FFD)
GRADS = (3 * DE, DE, FFE, DE, DD, 3 * DD, DD, FFD, DD)


def lookup(pos, tab, cols):
    row = lax.broadcasted_iota(jnp.int32, (48, 256), 0)
    spots = [jnp.concatenate([pos[0, i:i + 1, :], pos[1, i:i + 1, :]], axis=1) for i in range(3)]
    hot = jnp.logical_or(jnp.logical_or(row == spots[0], row == spots[1] + 16), row == spots[2] + 32)
    hot = jnp.where(hot, 1.0, 0.0).astype(jnp.bfloat16)
    return sum(dot_tn(hot, tab[i, :, cols]) for i in range(3))


def tile_mask(tile):
    ids = tile[lax.axis_index("tensor")]
    tiles = jnp.where(lax.broadcasted_iota(jnp.int32, (16, 256), 0) == ids, 1.0, 0.0).astype(jnp.bfloat16)
    return (1.0 - dot_tn(tiles, tiles)) * MASK_FILL


FWD_ACTS = [((256, n), jnp.bfloat16) for n in (DE, DE, DE, FFE)]
FWD_KEPT = [((256, 3 * DE), jnp.bfloat16), ((HE, 256, 256), jnp.float32), ((2, DE // 2, DE), jnp.bfloat16),
            ((256, DE), jnp.float32), ((256, 128), jnp.float32), ((256, DE), jnp.float32), ((256, 128), jnp.float32),
            ((256, FFE), jnp.float32)]


def chain_kernel(table, pos, tile, gains, biases, cot, tab, x2, w_hbm, *refs):
    fwd_hbm, refs = refs[:8], refs[8:]
    dec, dx0, norm_out = refs[:3]
    kept_out = refs[3:17]
    kept = refs[17:31]
    low, n1d, ad, n2d, ud, dpe, r1e, dhe, re, dlow, dpd, r1d, dhd, rd = kept
    fwd, refs = refs[31:39], refs[39:]
    proj_e, pe, ow_e, m1e, i1e, m2e, i2e, se = fwd
    (w, pd, sd, proj_d, da_e, da_d, ow_d, m1d, m2d, i1d, i2d, y, acc_e, acc_d, w_sem, f_sem, out_sem) = refs
    enc_b = Block(DE, HE, HDE, FFE, 0, table, 0)
    dec_b = Block(DD, HD, HDD, FFD, 5, table, DE)
    em = table[4]

    def load(m):
        rows = pl.ds(table[m][4], table[m][1] * table[m][5])
        return pltpu.make_async_copy(w_hbm.at[:, :, rows], w.at[:, :, rows], w_sem.at[m])

    def fetch(i):
        return pltpu.make_async_copy(fwd_hbm[i], fwd[i], f_sem.at[i])

    def store(i):
        return pltpu.make_async_copy(kept[i], kept_out[i], out_sem.at[i])

    for m in (4, 5, 6, 7, 8, 3, 2, 1, 0):
        if m != 1:
            load(m).start()
    for i in range(8):
        fetch(i).start()
    same = tile_mask(tile)
    low[...] = x2[...].astype(jnp.bfloat16)
    store(0).start()
    load(4).wait()
    for g in range(2):
        v = dot(low[...], pair(w, em, g)).astype(jnp.bfloat16).astype(jnp.float32)
        y[:, g * 128:(g + 1) * 128] = v[:, :128]
        y[:, 256 + g * 128:256 + (g + 1) * 128] = v[:, 128:]
    y[...] += lookup(pos, tab, slice(DE, DE + DD))
    for _ in block_fwd(dec_b, y, dec, w, gains, biases, same, n1d, proj_d, pd, ad, ow_d, m1d, i1d, n2d, m2d, i2d, ud, sd,
                       lambda k: load(5 + k).wait(), lambda k: store(1 + k).start()):
        pass
    y[...] = cot[...]
    block_bwd(dec_b, y, w, gains, same, n1d, proj_d, pd, ad, ow_d, m1d, i1d, n2d, m2d, i2d, ud, sd,
              rd, dhd, r1d, dpd, acc_d, da_d, norm_out, lambda k: store(10 + k).start())
    dlow[...] = y[...].astype(jnp.bfloat16)
    store(9).start()
    for g in range(2):
        d = jnp.concatenate([dlow[:, g * 128:(g + 1) * 128], dlow[:, 256 + g * 128:256 + (g + 1) * 128]], axis=1)
        v = dot_nt(d, pair(w, em, g))
        if g == 0:
            dx0[...] = v
        else:
            dx0[...] += v
    for m in (3, 2, 0):
        load(m).wait()
    for i in range(8):
        fetch(i).wait()
    block_bwd(enc_b, dx0, w, gains, same, None, proj_e, pe, None, ow_e, m1e, i1e, None, m2e, i2e, None, se,
              re, dhe, r1e, dpe, acc_e, da_e, norm_out, lambda k: store(5 + k).start())
    for i in range(14):
        store(i).wait()


def chain(pos, tile, gains, biases, cot, full, x2, fwd, table):
    f32, bf16 = jnp.float32, jnp.bfloat16
    S = jax.ShapeDtypeStruct
    outs = [S((256, DD), f32), S((256, DE), f32), S((4, DE + DD), f32)]
    kept = [(256, n) for n in ACTS[4:] + GRADS]
    outs += [S(k, bf16) for k in kept]
    V = pltpu.VMEM
    scratch = [V(k, bf16) for k in kept] + [V(k, t) for k, t in FWD_KEPT] + [
        V((2, 16) + full.shape[-2:], bf16), V((HD, 256, 256), f32), V((256, FFD), f32),
        V((256, 3 * DD), bf16), V((256, DE), bf16), V((256, DD), bf16), V((2, DD // 2, DD), bf16),
        V((256, DD), f32), V((256, DD), f32), V((256, 128), f32), V((256, 128), f32),
        V((256, DD), f32), V((256, DE), f32), V((256, DD), f32),
        pltpu.SemaphoreType.DMA((9,)), pltpu.SemaphoreType.DMA((8,)), pltpu.SemaphoreType.DMA((14,))]
    vmem = pl.BlockSpec(memory_space=pltpu.VMEM)
    hbm = pl.BlockSpec(memory_space=pl.ANY)
    args = (pos, tile, gains, biases, cot, jnp.asarray(position_table()), x2,
            full.reshape(2, 16, full.shape[-2], 128), *fwd)
    return pl.pallas_call(
        partial(chain_kernel, table), out_shape=outs, in_specs=[vmem] * 7 + [hbm] * 9, out_specs=[vmem] * 3 + [hbm] * 14,
        scratch_shapes=scratch, compiler_params=pltpu.CompilerParams(vmem_limit_bytes=63 << 20), name="chain",
        cost_estimate=pl.CostEstimate(flops=8_000_000_000, bytes_accessed=40_000_000, transcendentals=3_000_000),
    )(*args)


def grad_panels(table, m, act, grad, turned, put):
    mat = table[m]
    rb, panels, padded = mat[0], mat[1], mat[5]
    count = act.shape[1]

    def turn(i):
        turned[pl.ds(pl.multiple_of(i * 128, 128), 128), :] = act[:, lanes(i)].T

    repeat(count // 128, 6, turn)

    def place(t, g, v):
        if padded > rb:
            v = v.reshape(16, rb, 128)
            v = jnp.concatenate([v, jnp.zeros((16, padded - rb, 128), jnp.float32)], axis=1).astype(jnp.bfloat16)
        else:
            v = v.astype(jnp.bfloat16).reshape(16, rb, 128)
        put(t, g, v)

    if m in BY_ROWS:
        half = count // 2

        def body(i):
            t, g = i // (panels // 2), i % (panels // 2)
            v = dot(turned[pl.ds(pl.multiple_of(t * half, 128), half), :], grad[:, lanes(g, 256)])
            place(t, 2 * g, v[:, :128])
            place(t, 2 * g + 1, v[:, 128:])

        repeat(panels, 6, body)
    else:
        def body(g):
            d = jnp.concatenate([grad[:, lanes(g)], grad[:, lanes(panels + g)]], axis=1)
            v = dot(turned[:count, :], d)
            place(0, g, v[:, :128])
            place(1, g, v[:, 128:])

        repeat(panels, 6, body)


class Wires:
    def __init__(self, place, sem):
        self.place, self.sem, self.used, self.waits = place, sem, 0, []

    def new(self, n=1):
        self.used += n
        assert self.used <= self.sem.shape[0], self.used
        return self.used - n

    def copy(self, k, src, dst, way):
        return pltpu.make_async_remote_copy(src_ref=src, dst_ref=dst, send_sem=self.sem.at[k], recv_sem=self.sem.at[k + 1],
                                            device_id=self.place.ids[way], device_id_type=MESH)

    def send(self, k, src, dst, way, cond=None):
        cp = self.copy(k, src, dst, way)
        when(cond, cp.start)
        self.waits.append((cond, cp))

    def land(self, k, dst, cond=None):
        when(cond, self.copy(k, dst, dst, "c").wait_recv)

    def drain(self):
        for cond, cp in self.waits:
            when(cond, cp.wait_send)


def edge_slots(order):
    slots, used, shared = {}, 0, {}
    for d, kids in sorted(spread(order).items()):
        for _, way in kids:
            if way in "xy" and order.index("z") < order.index(way):
                key = (way, d[1], d[2])
                if key not in shared:
                    shared[key] = used
                    used += 4
                slots[d, way] = (shared[key], 4)
            else:
                slots[d, way] = (used, 1)
                used += 1
    return slots, used


def beyond(p, way):
    return p.z < 3 if way == "z+" else p.z > 0 if way == "z-" else None


def reduce_events(p, w, order, own, half, bufs, ready, done):
    tree = spread(order)
    pair = {d: w.new(2) for d in tree}
    wire = {d: w.new(2) for d in tree}
    parent = {nd: (d, way) for d, t in tree.items() for nd, way in t}
    slots, _ = edge_slots(order)

    def buffer(up, way):
        first, n = slots[up, way]
        return bufs.at[first + p.z + up[0] if n > 1 else first]

    events = []
    far = sorted(tree, key=lambda d: (-hops(d), d))
    for d in far:
        def act(d=d):
            cond = p.there(d)

            def step():
                acc = own(d)
                ready(d)
                w.land(pair[d], half(d))
                add_rows(acc, half(d))
                for nd, way in tree[d]:
                    buf = buffer(d, way)

                    def take(buf=buf, nd=nd):
                        w.land(wire[nd], buf)
                        add_rows(acc, buf)
                    when(beyond(p, way), take)
            when(cond, step)
            if hops(d) == 0:
                done()
            else:
                up, way = parent[d]
                w.send(wire[d], own(d), buffer(up, way), BACK[way], cond)
        events.append(act)

    def share(give):
        for d in far:
            w.send(pair[d], give(d), half(d), "c", p.there(d))

    return events, share, far


def gather_events(p, w, order, first, at):
    tree = spread(order)
    pair = {d: w.new(2) for d in tree}
    wire = {d: w.new(2) for d in tree}
    events = []
    for d in sorted(tree, key=lambda d: (hops(d), d)):
        def act(d=d):
            cond = p.there(d)
            blk = at(d, p.c)
            if hops(d):
                w.land(wire[d], blk, cond)
                src = blk
            else:
                src = first
            for nd, way in tree[d]:
                w.send(wire[nd], src, blk, way, both(cond, beyond(p, way)))
            w.send(pair[d], src, blk, "c", cond)
        events.append(act)

    def finish():
        for d in tree:
            w.land(pair[d], at(d, 1 - p.c), p.there(d))

    return events, finish


def run_events(lists, order, extra=iter(()), every=8):
    assert sorted(order) == sorted(64 * g + i for g, acts in enumerate(lists) for i in range(len(acts)))
    for n, k in enumerate(order):
        if n % every == 0:
            next(extra, None)
        lists[k // 64][k % 64]()
    for _ in extra:
        pass


def group_span(table, mats):
    first, last = table[mats[0]], table[mats[-1]]
    units = last[3] + last[2] - first[3]
    return first[3], -(-units // 16) * 16, first[4], last[4] + last[1] * last[5] - first[4]


def units_to_panels(table, mats, units, flat, put):
    base, count = table[mats[0]][3], units.shape[0]
    for k in range(4):
        flat[pl.ds(k, count, stride=4), :] = units[:, 128 * k:128 * (k + 1)].astype(jnp.float32)
    for m in mats:
        rb, panels, n, first, _, padded, _ = table[m]
        for g in range(panels):
            v = flat[pl.ds(4 * (first - base) + g, rb, stride=panels), :]
            if padded > rb:
                v = jnp.concatenate([v, jnp.zeros((padded - rb, 128), jnp.float32)], axis=0)
            put(m, g, v.astype(jnp.bfloat16))


def panels_to_units(table, mats, take, flat, units):
    base, count = table[mats[0]][3], units.shape[0]
    used = 0
    for m in mats:
        rb, panels, n, first, _, padded, _ = table[m]
        for g in range(panels):
            flat[pl.ds(4 * (first - base) + g, rb, stride=panels), :] = take(m, g)[:rb]
        used = 4 * (first - base + n)
    if used < 4 * count:
        flat[used:4 * count, :] = jnp.zeros((4 * count - used, 128), jnp.float32)
    for k in range(4):
        units[:, 128 * k:128 * (k + 1)] = flat[pl.ds(k, count, stride=4), :].astype(jnp.bfloat16)


def encoder_steps(p, table, out, tok, pos, x, x2, tile, gains, biases, tab, fwd, fwd_out, wv, w_sem, fwd_sem, swapped, arrived):
    n1, att, n2, act, proj, prob, ow, m1, i1, m2, i2, slope = fwd

    def load(m):
        rows = pl.ds(table[m][4], table[m][1] * table[m][5])
        return pltpu.make_async_copy(out.at[:, :, :, :, rows], wv.at[:, :, :, :, rows], w_sem.at[m])

    def store(i):
        return pltpu.make_async_copy(fwd[i], fwd_out[i], fwd_sem.at[i])

    for f in swapped:
        f()
    x[...] = tok[...].reshape(256, DE).astype(jnp.float32) + lookup(pos, tab, slice(0, DE))
    same = tile_mask(tile)
    whole = wv.reshape(2, 16, wv.shape[-2], 128)
    block = block_fwd(Block(DE, HE, HDE, FFE, 0, table, 0), x, x2, whole, gains, biases, same, n1, proj, prob, att, ow, m1, i1, n2,
                      m2, i2, act, slope, lambda k: load(k).wait(), lambda k: store(k).start())
    next(block)
    yield
    for f in arrived[0]:
        f()
    load(0).start()
    load(1).start()
    yield
    for _ in range(4):
        next(block)
        yield
    for f in arrived[1]:
        f()
    load(2).start()
    yield
    next(block)
    yield
    for f in arrived[2]:
        f()
    load(3).start()
    yield
    for _ in block:
        pass
    for i in range(4, 12):
        store(i).start()
    yield
    for i in range(12):
        store(i).wait()


class Swap:
    def __init__(self, p, w, src, out, give, keep):
        self.p, self.w, self.src, self.out, self.give, self.keep = p, w, src, out, give, keep
        self.k, self.own = w.new(2), w.new()

    def local(self):
        return pltpu.make_async_copy(self.src.at[self.keep], self.out.at[self.p.x], self.w.sem.at[self.own])

    def start(self):
        self.w.send(self.k, self.src.at[self.give], self.out.at[self.p.x], "x")
        self.local().start()

    def finish(self):
        self.w.land(self.k, self.out.at[1 - self.p.x])
        self.local().wait()


def weights_kernel(table, groups, plan, parts, tok_in, pos_in, cot_in, tile, gains, biases, tab, *refs):
    n = len(groups)
    out, pos, cot, x2 = refs[:4]
    fwd_out, tok, x, fwd, wv, w_sem, fwd_sem = refs[4:16], refs[16], refs[17], refs[18:30], refs[30], refs[31], refs[32]
    rest = refs[33:]
    accs, halves, bufs, shards = (rest[i * n:(i + 1) * n] for i in range(4))
    flat, sem = rest[4 * n:]
    p = Place()
    p.greet(["c", "y", "x"])
    w = Wires(p, sem)
    swaps = [Swap(p, w, a, b, 1 - p.x, p.x) for a, b in ((tok_in, tok), (pos_in, pos), (cot_in, cot))]
    for s in swaps:
        s.start()
    lists, finishes = [], []
    for g, mats in enumerate(groups):
        u0, un, r0, rn = group_span(table, mats)
        acc, half, buf, shard = accs[g], halves[g], bufs[g], shards[g]
        own_sem = w.new()
        loads = {d: w.new() for d in spread(plan[0][g])}

        def own(d, acc=acc):
            return acc.at[p.at(d)[1:]]

        def other(d, half=half):
            return half.at[p.at(d)[1:]]

        def load(d, u0=u0, un=un, own=own, loads=loads):
            return pltpu.make_async_copy(parts.at[p.at(d)[1:] + (p.c, pl.ds(u0, un))], own(d), sem.at[loads[d]])

        def ready(d, load=load):
            load(d).wait()

        def done(mats=mats, acc=acc, shard=shard, r0=r0):
            def put(m, i, v):
                lo = table[m][4] - r0 + i * table[m][5]
                shard[lo:lo + table[m][5], :] = v
            units_to_panels(table, mats, acc.at[p.z, p.y], flat, put)

        ev, share, far = reduce_events(p, w, plan[0][g], own, other, buf, ready, done)

        def begin(load=load, share=share, far=far, u0=u0, un=un):
            share(lambda d: parts.at[p.at(d)[1:] + (1 - p.c, pl.ds(u0, un))])
            for d in far:
                when(p.there(d), load(d).start)

        def at(d, core, r0=r0, rn=rn):
            t, z, y = p.at(d)
            return out.at[t, z, y, core, pl.ds(r0, rn)]

        def local(shard=shard, r0=r0, rn=rn, own_sem=own_sem):
            return pltpu.make_async_copy(shard, out.at[p.x, p.z, p.y, p.c, pl.ds(r0, rn)], sem.at[own_sem])

        ag, finish = gather_events(p, w, plan[1][g], shard, at)

        def send_first(act=ag[0], local=local):
            act()
            local().start()

        lists.append([begin] + ev + [send_first] + ag[1:])
        finishes += [finish, lambda local=local: local().wait()]
    steps = encoder_steps(p, table, out, tok, pos, x, x2, tile, gains, biases, tab, fwd, fwd_out, wv, w_sem, fwd_sem,
                          [s.finish for s in swaps[:2]], [finishes[2 * k:2 * k + 2] for k in range(3)])
    lists.append([partial(next, steps, None)] * 11)
    run_events(lists, plan[2])
    for f in finishes[6:] + [swaps[2].finish]:
        f()
    w.drain()


def spread_weights(parts, tokens, pos, cot, tile, gains, biases, table, rows, groups, plan, ident):
    spans = [group_span(table, m) for m in groups]
    bf16 = jnp.bfloat16
    S = jax.ShapeDtypeStruct
    V = pltpu.VMEM
    fwd = FWD_ACTS + FWD_KEPT
    enc_rows = table[4][4]
    scratch = [V(tokens.shape, tokens.dtype), V((256, DE), jnp.float32)] + [V(k, t) for k, t in fwd]
    scratch += [V((2, 4, 2, 2, enc_rows, 128), bf16), pltpu.SemaphoreType.DMA((4,)), pltpu.SemaphoreType.DMA((12,))]
    scratch += [V((4, 2, s[1], 512), bf16) for s in spans] * 2
    scratch += [V((edge_slots(o)[1], s[1], 512), bf16) for s, o in zip(spans, plan[0])]
    scratch += [V((s[3], 128), bf16) for s in spans]
    scratch += [V((4 * max(s[1] for s in spans), 128), jnp.float32),
                pltpu.SemaphoreType.DMA((len(groups) * (1 + 5 * 14 + 4 * 28) + 9,))]
    hbm = pl.BlockSpec(memory_space=pl.ANY)
    vmem = pl.BlockSpec(memory_space=pltpu.VMEM)
    return pl.pallas_call(
        partial(weights_kernel, table, groups, plan),
        out_shape=[S((2, 4, 2, 2, rows, 128), bf16), S(pos.shape, pos.dtype), S(cot.shape, cot.dtype), S((256, DE), jnp.float32)]
        + [S(k, t) for k, t in fwd],
        in_specs=[hbm] * 4 + [vmem] * 4, out_specs=[hbm, vmem, hbm, vmem] + [hbm] * 12,
        scratch_shapes=scratch,
        compiler_params=pltpu.CompilerParams(collective_id=ident, has_side_effects=True, vmem_limit_bytes=63 << 20),
        name="spread_weights",
    )(parts, tokens, pos, cot, tile, gains, biases, jnp.asarray(position_table()))


def return_kernel(table, groups, plan, *refs):
    n = len(groups)
    kept_in, small_src, dec_in, dx_in, out, small_out, dec, dx = refs[:18], *refs[18:25]
    rest = refs[25:]
    kept, rest = rest[:18], rest[18:]
    acts, grads = kept[:9], kept[9:]
    sides, halves, bufs, units = (rest[i * n:(i + 1) * n] for i in range(4))
    flat, turned, mid, line, load_sem, sem = rest[4 * n:]

    def load(i):
        return pltpu.make_async_copy(kept_in[i], kept[i], load_sem.at[i])

    first = sorted(range(n), key=lambda g: plan[2].index(64 * g))
    for g in first:
        for m in groups[g]:
            load(m).start()
            load(9 + m).start()
    p = Place()
    p.greet(["c", "y", "x"])
    w = Wires(p, sem)
    swaps = [Swap(p, w, a, b, 1 - p.x, p.x) for a, b in ((dec_in, dec), (dx_in, dx))]
    swaps[0].start()
    lists, finishes = [], []
    for g, mats in enumerate(groups):
        u0, un, r0, rn = group_span(table, mats)
        side, half, buf, unit = sides[g], halves[g], bufs[g], units[g]
        own_sem = w.new()

        def own(d, side=side):
            return side.at[(p.c,) + p.at(d)]

        def other(d, half=half):
            return half.at[p.at(d)]

        def done(mats=mats, side=side, unit=unit, r0=r0):
            mine = side.at[p.c, p.x, p.z, p.y]

            def take(m, i):
                lo = table[m][4] - r0 + i * table[m][5]
                return mine[lo:lo + table[m][5], :].astype(jnp.float32)
            panels_to_units(table, mats, take, flat, unit)

        ev, share, far = reduce_events(p, w, plan[0][g], own, other, buf, lambda d: None, done)

        def begin(mats=mats, side=side, share=share, r0=r0):
            for m in mats:
                lo, padded = table[m][4] - r0, table[m][5]

                def put(t, i, v, lo=lo, padded=padded):
                    v = v.reshape(4, 2, 2, padded, 128)
                    rows = pl.ds(pl.multiple_of(lo + i * padded, 16), padded)
                    side[0, t, :, :, rows, :] = v[:, :, 0]
                    side[1, t, :, :, rows, :] = v[:, :, 1]
                load(m).wait()
                load(9 + m).wait()
                grad_panels(table, m, acts[m], grads[m], turned, put)
            share(lambda d: side.at[(1 - p.c,) + p.at(d)])

        def at(d, core, u0=u0, un=un):
            _, z, y = p.at(d)
            return out.at[z, y, core, pl.ds(u0, un)]

        def local(unit=unit, u0=u0, un=un, own_sem=own_sem):
            return pltpu.make_async_copy(unit, out.at[p.z, p.y, p.c, pl.ds(u0, un)], sem.at[own_sem])

        ag, finish = gather_events(p, w, plan[1][g], unit, at)

        def send_first(act=ag[0], local=local):
            act()
            local().start()

        lists.append([begin] + ev + [send_first] + ag[1:])
        finishes += [finish, lambda local=local: local().wait()]
    last = max(plan[2].index(64 * g + len(spread(plan[0][g]))) for g in range(n))
    g, i = plan[2][last] // 64, plan[2][last] % 64
    act = lists[g][i]

    def with_swaps():
        act()
        swaps[1].start()

    lists[g][i] = with_swaps
    run_events(lists, plan[2], total_steps(p, w, small_src, small_out, mid, line))
    for f in finishes + [s.finish for s in swaps]:
        f()
    w.drain()


def total_steps(p, w, src, out, mid, line):
    k = [w.new(2) for _ in range(9)]
    now = src
    for i, way in enumerate(("c", "x", "y")):
        w.send(k[i], now, mid.at[i], way)
        yield
        w.land(k[i], mid.at[i])
        nxt = mid.at[3 + i] if i < 2 else line.at[p.z]
        nxt[...] = now[...] + mid[i]
        now = nxt
    for i in range(4):
        lo, hi = jnp.maximum(p.z - i, 0), jnp.minimum(p.z + i, 3)
        if i > 0:
            w.land(k[2 + i], line.at[lo], p.z >= i)
            w.land(k[5 + i], line.at[hi], p.z + i <= 3)
        if i < 3:
            w.send(k[3 + i], line.at[lo], line.at[lo], "z+", jnp.logical_and(p.z >= i, p.z < 3))
            w.send(k[6 + i], line.at[hi], line.at[hi], "z-", jnp.logical_and(p.z + i <= 3, p.z > 0))
            yield
    out[...] = (line[0] + line[1]) + (line[2] + line[3])


def return_grads(kept, small, dec, dx, table, total_units, groups, plan, ident):
    spans = [group_span(table, m) for m in groups]
    bf16 = jnp.bfloat16
    S = jax.ShapeDtypeStruct
    V = pltpu.VMEM
    scratch = [V(v.shape, v.dtype) for v in kept]
    scratch += [V((2, 2, 4, 2, s[3], 128), bf16) for s in spans]
    scratch += [V((2, 4, 2, s[3], 128), bf16) for s in spans]
    scratch += [V((edge_slots(o)[1], s[3], 128), bf16) for s, o in zip(spans, plan[0])]
    scratch += [V((s[1], 512), bf16) for s in spans]
    scratch += [V((4 * max(s[1] for s in spans), 128), jnp.float32), V((FFE, 256), bf16),
                V((5,) + small.shape, small.dtype), V((4,) + small.shape, small.dtype), pltpu.SemaphoreType.DMA((18,)),
                pltpu.SemaphoreType.DMA((len(groups) * (1 + 4 * 14 + 4 * 28) + 24,))]
    vmem = pl.BlockSpec(memory_space=pltpu.VMEM)
    hbm = pl.BlockSpec(memory_space=pl.ANY)
    return pl.pallas_call(
        partial(return_kernel, table, groups, plan),
        out_shape=(S((4, 2, 2, total_units, 512), bf16), S(small.shape, small.dtype), S(dec.shape, dec.dtype), S(dx.shape, dx.dtype)),
        in_specs=[hbm] * 18 + [vmem, hbm, hbm], out_specs=(hbm, vmem, hbm, hbm),
        scratch_shapes=scratch,
        compiler_params=pltpu.CompilerParams(collective_id=ident, has_side_effects=True, vmem_limit_bytes=63 << 20),
        name="return_grads",
    )(*kept, small, dec, dx)


STEP_ROWS = 432


def update_kernel(place_s, place, spread, master, first, second, total, params, norm_first, norm_second,
                  new_master, new_first, new_second, new_norms, new_nf, new_ns):
    i = pl.program_id(0)

    @pl.when(i == 0)
    def _():
        new_norms[...], new_nf[...], new_ns[...] = adamw(params[...], total[...], norm_first[...], norm_second[...], 0.0, NORM_RATE)

    lane = lax.broadcasted_iota(jnp.int32, (16, 256), 1)
    row = lax.broadcasted_iota(jnp.int32, (16, 256), 0)
    for k in range(STEP_ROWS // 16):
        tiles = []
        for j in range(16):
            at = jnp.minimum(place_s[i * STEP_ROWS + 16 * k + j] >> 4, spread.shape[0] // 16 - 1)
            tiles.append(spread[pl.ds(pl.multiple_of(at * 16, 16), 16), :])
        here = slice(16 * k, 16 * k + 16)
        spot = place[here, :]
        used = jnp.logical_and(lane == row * 16 + (spot & 15), spot < spread.shape[0])
        grad = dot(jnp.where(used, 1.0, 0.0).astype(jnp.bfloat16), jnp.concatenate(tiles, axis=0))
        new_master[here, :], new_first[here, :], new_second[here, :] = adamw(
            master[here, :], grad, first[here, :], second[here, :], WEIGHT_DECAY, LEARN_RATE)


def update(place, spread, master, first, second, total, params, norm_first, norm_second):
    slots = master.shape[0]
    S = jax.ShapeDtypeStruct
    rows = pl.BlockSpec((STEP_ROWS, 512), lambda i, s: (i, 0))
    whole = lambda v: pl.BlockSpec(v.shape, lambda i, s: (0, 0), pipeline_mode=pl.Buffered(1))
    small = pl.BlockSpec(params.shape, lambda i, s: (0, 0))
    out = [S(master.shape, jnp.float32)] * 3 + [S(params.shape, jnp.float32)] * 3
    return pl.pallas_call(
        update_kernel, out_shape=out,
        grid_spec=pltpu.PrefetchScalarGridSpec(
            num_scalar_prefetch=1, grid=(slots // STEP_ROWS,),
            in_specs=[pl.BlockSpec((STEP_ROWS, 1), lambda i, s: (i, 0)), whole(spread), rows, rows, rows, small, small, small, small],
            out_specs=[rows] * 3 + [small] * 3),
        compiler_params=pltpu.CompilerParams(vmem_limit_bytes=62 << 20), name="update",
    )(place, lax.optimization_barrier(place)[:, None], spread, master, first, second, total, params, norm_first, norm_second)


def place_kernel(place_s, master, out, wide, staged, sem):
    count = wide.shape[0] // 64 - 1

    def clear(i, _):
        wide[pl.ds(pl.multiple_of(i * 64, 64), 64), :] = jnp.zeros((64, 512), jnp.float32)
        return 0

    lax.fori_loop(0, count, clear, 0)

    def turn(i, _):
        for j in range(16):
            wide[pl.ds(place_s[i * 16 + j], 1), :] = master[pl.ds(i * 16 + j, 1), :]
        return 0

    lax.fori_loop(0, master.shape[0] // 16, turn, 0)
    parts = 4
    part = count // parts * 64

    def copy(k):
        rows = pl.ds(pl.multiple_of(k * part, 64), part)
        return pltpu.make_async_copy(staged.at[rows], out.at[rows], sem.at[k])

    for k in range(parts):
        def narrow(i, _):
            rows = pl.ds(pl.multiple_of(k * part + i * 64, 64), 64)
            staged[rows, :] = wide[rows, :].astype(jnp.bfloat16)
            return 0

        lax.fori_loop(0, part // 64, narrow, 0)
        copy(k).start()
    for k in range(parts):
        copy(k).wait()


def place_blocks(place, master, rows):
    return pl.pallas_call(
        place_kernel, out_shape=jax.ShapeDtypeStruct((rows, 512), jnp.bfloat16),
        grid_spec=pltpu.PrefetchScalarGridSpec(
            num_scalar_prefetch=1, grid=(1,),
            in_specs=[pl.BlockSpec(master.shape, lambda i, s: (0, 0), pipeline_mode=pl.Buffered(1))],
            out_specs=pl.BlockSpec(memory_space=pl.ANY),
            scratch_shapes=[pltpu.VMEM((rows + 64, 512), jnp.float32), pltpu.VMEM((rows, 512), jnp.bfloat16), pltpu.SemaphoreType.DMA((4,))]),
        compiler_params=pltpu.CompilerParams(vmem_limit_bytes=60 << 20), name="place_blocks",
    )(place, master)


def sequence_device(tokens_in, positions, segment_ids, owners, master, first_moment, second_moment, norm_gains,
                    norm_biases, norm_first, norm_second, cotangent):
    shapes = weight_shapes(2)
    table, _, rows = layout(shapes, 16)
    unit, used = own_units(owners, lax.axis_index("dp"), master.shape[0])
    place = jnp.where(used, unit_places(unit, table, 16), 16 * SHARD_UNITS)
    parts = place_blocks(place, master, 16 * SHARD_UNITS)
    full, pos, cot, x2, *fwd = spread_weights(parts.reshape(4, 2, 2, SHARD_UNITS, 512), tokens_in, positions.transpose(1, 0, 2),
                                              cotangent, segment_ids, norm_gains, norm_biases, table, rows, GROUPS, PLAN_OUT, 1)
    kept = chain(pos, segment_ids, norm_gains, norm_biases, cot.reshape(256, DD), full, x2, fwd[4:], table)
    decoded, dx0, norms = kept[:3]
    spread_out, norm_total, decoded, dx0 = return_grads([*fwd[:4], *kept[3:]], norms, decoded.reshape(2, 128, DD), dx0.reshape(2, 128, DE), table,
                                                        SHARD_UNITS, GROUPS, PLAN_BACK, 2)
    norm_params = jnp.concatenate([norm_gains, norm_biases], axis=0)
    new_master, new_first, new_second, new_norms, norm_one_new, norm_two_new = update(
        place, spread_out.reshape(16 * SHARD_UNITS, 512), master, first_moment, second_moment, norm_total, norm_params, norm_first, norm_second)
    return (decoded, dx0, new_master, new_first, new_second, new_norms, norm_one_new, norm_two_new)


def solution(mesh):
    step = sequence_device if (mesh.shape["dp"], mesh.shape["tensor"]) == (16, 2) else per_device
    return jax.shard_map(
        step,
        mesh=mesh,
        in_specs=(
            P(None, ("dp", "tensor"), None),
            P(None, None, ("dp", "tensor")),
            P(None, "dp", None),
            P(),
            P("dp", "tensor"),
            P("dp", "tensor"),
            P("dp", "tensor"),
            P(),
            P(),
            P(),
            P(),
            P(None, ("dp", "tensor"), None),
        ),
        out_specs=(
            P(None, ("dp", "tensor"), None),
            P(None, ("dp", "tensor"), None),
            P("dp", "tensor"),
            P("dp", "tensor"),
            P("dp", "tensor"),
            P(),
            P(),
            P(),
        ),
        check_vma=False,
    )
```

profile of v0, /device:TPU:1, one launch (start us, length us, event | category | flops | bytes accessed | tf_op | source)
XLA Modules:
  0.0 340.7 jit_solution(17840962420676938503)
XLA Ops:
  0.6 0.9 compare_reduce_fusion
  1.5 0.1 fusion.3
  1.7 0.2 fusion.4
  1.9 0.1 select_reduce_fusion.1
  2.0 0.1 convert_reduce_fusion
  2.2 0.2 select_reduce_fusion
  2.3 0.7 fusion.1
  3.0 0.6 slice.7
  3.6 1.3 fusion.11.place_s
  4.9 0.0 copy-start.5
  4.9 13.3 %place_blocks.1 = bf16[10496,512]{1,0:T(8,128)(2,1)} custom-call(s32[1296]{0:T(1024)} %fusion.11.place_s, f32[1296,512]{1,0:T(8,128)} %master.3), custom_call_target="tpu_custom_call" | custom-call | tf_op jit(solution)/shard_map/place_blocks/pallas_call | solution.py:1507
  18.3 0.0 copy-done.5
  18.3 0.6 copy.28
  18.9 140.4 %spread_weights.1 = (bf16[2,4,2,2,2640,128]{5,4,3,2,1,0:T(8,128)(2,1)}, s32[2,3,128]{2,1,0:T(4,128)}, f32[2,128,512]{2,1,0:T(8,128)}, f32[256,768]{1,0:T(8,128)}...) custom-call(bf16[4,2,2,656,512]{4,3,2,1,0:T(8,128)(2,1)} %bitcast.13, ...), custom_call_target="tpu_custom_call" | custom-call | tf_op jit(solution)/shard_map/spread_weights/pallas_call | solution.py:1283
  159.3 30.8 %chain.1 = (f32[256,512]{1,0:T(8,128)}, f32[256,768]{1,0:T(8,128)}, f32[4,1280]{1,0:T(4,128)}, bf16[256,768]{1,0:T(8,128)(2,1)}, bf16[256,512]{1,0:T(8,128)(2,1)...) custom-call(s32[2,3,128]{2,1,0:T(4,128)} %get-tuple-element.55.pos, ...), custom_call_target="tpu_custom_call" | custom-call | flops 8000000000 | bytes 40000000 | tf_op jit(solution)/shard_map/chain/pallas_call | solution.py:931
  190.0 0.0 copy-start.2
  190.1 0.0 copy-start.3
  190.1 0.0 copy-start.4
  190.1 132.8 %return_grads.1 = (bf16[4,2,2,656,512]{4,3,2,1,0:T(8,128)(2,1)}, f32[4,1280]{1,0:T(4,128)}, f32[2,128,512]{2,1,0:T(8,128)}, f32[2,128,768]{2,1,0:T(8,128)}) custom-call(bf16[256,768]{1,0:T(8,128)(2,1)} %get-tuple-element.51.refs_0_, bf16[256,768]{1,0:T(8,128)(2,1)} %get-tuple-element.52.refs_1_, bf16[256,768]{1,0:T(8,128)(2,1)} %get-tuple-element.53.refs_2_, ...), custom_call_target="tpu_custom_call" | custom-call | tf_op jit(solution)/shard_map/return_grads/pallas_call | solution.py:1419
  322.9 0.0 copy-done.2
  322.9 1.1 broadcast_in_dim.48.place
  323.9 0.0 copy-done.3
  323.9 0.0 copy-done.4
  323.9 0.6 pad_maximum_fusion.params
  324.6 0.0 copy-start.1
  324.6 0.0 copy-start
  324.6 14.0 %update.1 = (f32[1296,512]{1,0:T(8,128)}, f32[1296,512]{1,0:T(8,128)}, f32[1296,512]{1,0:T(8,128)}, f32[4,1280]{1,0:T(4,128)}, f32[4,1280]{1,0:T(4,128)}, /*index=5*/f32[4,1280]{1,0:T(4,128)}) custom-call(s32[1296]{0:T(1024)} %fusion.11.place_s, s32[1296,1]{1,0:T(8,128)} %broadcast_in_dim.48.place, bf16[10496,512]{1,0:T(8,128)(2,1)} %bitcast.15, ...), custom_call_target="tpu_custom_call" | custom-call | tf_op jit(solution)/shard_map/update/pallas_call | solution.py:1462
  338.6 0.0 copy-done.1
  338.6 0.8 copy.31
  339.4 0.0 copy-done
  339.4 0.9 copy.32
  (2 shorter events, 0.0 us)
Async XLA Ops:
  4.9 13.3 %copy-start.5 = (s32[3,2,128]{2,1,0:T(2,128)S(1)}, s32[3,2,128]{2,1,0:T(2,128)}, u32[]{:S(2)}) copy-start(s32[3,2,128]{2,1,0:T(2,128)} %param.15) | copy-start | bytes 9220
  190.0 132.8 %copy-start.2 = (s32[1296]{0:T(1024)S(1)}, s32[1296]{0:T(1024)}, u32[]{:S(2)}) copy-start(s32[1296]{0:T(1024)} %fusion.11.place_s) | copy-start | bytes 15556
  190.1 133.9 %copy-start.3 = (f32[2,1280]{1,0:T(2,128)S(1)}, f32[2,1280]{1,0:T(2,128)}, u32[]{:S(2)}) copy-start(f32[2,1280]{1,0:T(2,128)} %gains.3) | copy-start | bytes 30724
  190.1 133.9 %copy-start.4 = (f32[2,1280]{1,0:T(2,128)S(1)}, f32[2,1280]{1,0:T(2,128)}, u32[]{:S(2)}) copy-start(f32[2,1280]{1,0:T(2,128)} %biases.3) | copy-start | bytes 30724
  324.6 14.0 %copy-start.1 = (f32[2,128,512]{2,1,0:T(8,128)S(1)}, f32[2,128,512]{2,1,0:T(8,128)}, u32[]{:S(2)}) copy-start(f32[2,128,512]{2,1,0:T(8,128)} %get-tuple-element.102) | copy-start | bytes 1572868
  324.6 14.8 %copy-start = (f32[2,128,768]{2,1,0:T(8,128)S(1)}, f32[2,128,768]{2,1,0:T(8,128)}, u32[]{:S(2)}) copy-start(f32[2,128,768]{2,1,0:T(8,128)} %get-tuple-element.103) | copy-start | bytes 2359300
where the time goes:
time: 347 us; the launch traced here: 341 us
  Pallas kernels  331 us (95%)
  local copies, waits for them, and re-layouts  3.96 us (1%)
    pallas_call x1, Pallas kernels, spread_weights(): pl.pallas_call(partial(weights_kernel, table, groups, plan), out_shape=[S...  140 us
    pallas_call x1, Pallas kernels, return_grads(): pl.pallas_call(partial(return_kernel, table, groups, plan), out_shape=(S(...  133 us
    pallas_call x1, Pallas kernels, chain(): pl.pallas_call(partial(chain_kernel, table), out_shape=outs, in_specs=[vm...  30.8 us
    pallas_call x1, Pallas kernels, update(): pl.pallas_call(update_kernel, out_shape=out, grid_spec=pltpu.PrefetchScal...  14 us
    pallas_call x1, Pallas kernels, place_blocks(): pl.pallas_call(place_kernel, out_shape=jax.ShapeDtypeStruct((rows, 512),...  13.3 us

commit v1 on v0

--- a/solution.py
+++ b/solution.py
@@ -491,19 +491,19 @@
 GROUPS = ((0, 1), (2,), (3,), (4, 5, 6), (7, 8))
 
 PLAN_OUT = (
-    ("zy", "zy", "yz", "yz", "yz"),
-    ("zxy", "yzx", "zyx", "yzx", "xzy"),
+    ("zy", "yz", "zy", "yz", "yz"),
+    ("zyx", "zxy", "zyx", "yzx", "xzy"),
     (
-        128, 129, 0, 4, 131, 130, 132, 8, 134, 64, 135, 133, 1, 9, 2, 68, 69, 5, 138, 137, 73, 256, 6, 136, 3, 192,
-        65, 140, 141, 66, 139, 7, 72, 10, 142, 143, 70, 12, 13, 67, 11, 147, 146, 144, 76, 71, 148, 74, 154, 14, 15,
-        75, 77, 16, 193, 257, 162, 258, 19, 78, 194, 79, 320, 259, 168, 260, 196, 26, 197, 261, 20, 156, 80, 83, 82,
-        262, 265, 198, 170, 155, 27, 145, 17, 151, 32, 84, 264, 86, 34, 200, 24, 157, 163, 266, 22, 90, 195, 28, 89,
-        160, 40, 29, 268, 202, 36, 201, 152, 85, 88, 263, 91, 21, 93, 269, 97, 199, 267, 92, 35, 33, 25, 104, 205, 81,
-        204, 203, 39, 270, 271, 167, 150, 206, 207, 23, 272, 31, 273, 101, 276, 37, 98, 210, 41, 100, 38, 42, 275,
-        278, 103, 18, 211, 161, 96, 149, 165, 30, 95, 164, 280, 208, 277, 321, 215, 322, 102, 282, 153, 212, 323, 290,
-        283, 94, 217, 106, 169, 279, 285, 209, 324, 87, 105, 158, 218, 216, 288, 289, 166, 99, 214, 159, 325, 225,
-        284, 219, 326, 226, 220, 292, 327, 227, 221, 291, 224, 213, 294, 295, 328, 230, 296, 228, 293, 281, 274, 232,
-        287, 223, 286, 329, 231, 222, 298, 297, 330, 233, 229, 234,
+        64, 65, 66, 0, 70, 1, 128, 2, 4, 5, 6, 137, 68, 3, 8, 9, 12, 7, 192, 130, 256, 140, 69, 10, 73, 129, 133, 136,
+        13, 11, 74, 72, 67, 262, 14, 15, 71, 134, 131, 77, 132, 19, 76, 18, 75, 16, 320, 26, 135, 24, 138, 20, 78, 79,
+        22, 141, 139, 195, 34, 257, 27, 81, 32, 193, 258, 25, 80, 35, 259, 83, 142, 143, 90, 30, 194, 266, 82, 196,
+        39, 40, 144, 199, 84, 197, 260, 198, 263, 148, 147, 200, 261, 264, 31, 201, 202, 203, 98, 33, 29, 28, 42, 91,
+        21, 155, 154, 36, 265, 204, 205, 269, 23, 268, 157, 267, 206, 164, 207, 86, 162, 17, 92, 103, 38, 88, 270, 37,
+        271, 41, 210, 106, 161, 104, 96, 85, 99, 146, 150, 321, 322, 275, 160, 272, 211, 323, 273, 89, 153, 324, 100,
+        101, 276, 208, 105, 168, 97, 165, 282, 217, 163, 218, 95, 209, 93, 87, 152, 214, 166, 325, 94, 151, 167, 102,
+        280, 169, 290, 326, 277, 327, 159, 170, 225, 145, 221, 226, 216, 149, 156, 279, 158, 288, 212, 284, 328, 283,
+        278, 228, 329, 295, 291, 213, 223, 219, 285, 232, 220, 330, 224, 296, 286, 292, 274, 289, 233, 230, 234, 229,
+        281, 287, 222, 227, 231, 215, 294, 293, 298, 297,
     ),
 )
 PLAN_BACK = (
@@ -1142,13 +1142,17 @@
     def store(i):
         return pltpu.make_async_copy(fwd[i], fwd_out[i], fwd_sem.at[i])
 
+    def keep(k):
+        for i in ((0, 7, 8), (1, 4, 5), (2, 6, 9, 10), (3, 11))[k]:
+            store(i).start()
+
     for f in swapped:
         f()
     x[...] = tok[...].reshape(256, DE).astype(jnp.float32) + lookup(pos, tab, slice(0, DE))
     same = tile_mask(tile)
     whole = wv.reshape(2, 16, wv.shape[-2], 128)
     block = block_fwd(Block(DE, HE, HDE, FFE, 0, table, 0), x, x2, whole, gains, biases, same, n1, proj, prob, att, ow, m1, i1, n2,
-                      m2, i2, act, slope, lambda k: load(k).wait(), lambda k: store(k).start())
+                      m2, i2, act, slope, lambda k: load(k).wait(), keep)
     next(block)
     yield
     for f in arrived[0]:
@@ -1171,8 +1175,6 @@
     yield
     for _ in block:
         pass
-    for i in range(4, 12):
-        store(i).start()
     yield
     for i in range(12):
         store(i).wait()
@@ -1429,12 +1431,16 @@
 STEP_ROWS = 432
 
 
-def update_kernel(place_s, place, spread, master, first, second, total, params, norm_first, norm_second,
-                  new_master, new_first, new_second, new_norms, new_nf, new_ns):
+def update_kernel(place_s, place, spread, master, first, second, total, params, norm_first, norm_second, *refs):
+    passed, refs = refs[:2], refs[2:]
+    new_master, new_first, new_second, new_norms, new_nf, new_ns = refs[:6]
     i = pl.program_id(0)
+    copies = [pltpu.make_async_copy(a, b, refs[8].at[k]) for k, (a, b) in enumerate(zip(passed, refs[6:8]))]
 
     @pl.when(i == 0)
     def _():
+        for c in copies:
+            c.start()
         new_norms[...], new_nf[...], new_ns[...] = adamw(params[...], total[...], norm_first[...], norm_second[...], 0.0, NORM_RATE)
 
     lane = lax.broadcasted_iota(jnp.int32, (16, 256), 1)
@@ -1451,22 +1457,28 @@
         new_master[here, :], new_first[here, :], new_second[here, :] = adamw(
             master[here, :], grad, first[here, :], second[here, :], WEIGHT_DECAY, LEARN_RATE)
 
-
-def update(place, spread, master, first, second, total, params, norm_first, norm_second):
+    @pl.when(i == pl.num_programs(0) - 1)
+    def _():
+        for c in copies:
+            c.wait()
+
+
+def update(place, spread, master, first, second, total, params, norm_first, norm_second, passed):
     slots = master.shape[0]
     S = jax.ShapeDtypeStruct
     rows = pl.BlockSpec((STEP_ROWS, 512), lambda i, s: (i, 0))
     whole = lambda v: pl.BlockSpec(v.shape, lambda i, s: (0, 0), pipeline_mode=pl.Buffered(1))
     small = pl.BlockSpec(params.shape, lambda i, s: (0, 0))
-    out = [S(master.shape, jnp.float32)] * 3 + [S(params.shape, jnp.float32)] * 3
+    out = [S(master.shape, jnp.float32)] * 3 + [S(params.shape, jnp.float32)] * 3 + [S(v.shape, v.dtype) for v in passed]
+    hbm = pl.BlockSpec(memory_space=pl.ANY)
     return pl.pallas_call(
         update_kernel, out_shape=out,
         grid_spec=pltpu.PrefetchScalarGridSpec(
             num_scalar_prefetch=1, grid=(slots // STEP_ROWS,),
-            in_specs=[pl.BlockSpec((STEP_ROWS, 1), lambda i, s: (i, 0)), whole(spread), rows, rows, rows, small, small, small, small],
-            out_specs=[rows] * 3 + [small] * 3),
+            in_specs=[pl.BlockSpec((STEP_ROWS, 1), lambda i, s: (i, 0)), whole(spread), rows, rows, rows, small, small, small, small, hbm, hbm],
+            out_specs=[rows] * 3 + [small] * 3 + [hbm, hbm], scratch_shapes=[pltpu.SemaphoreType.DMA((2,))]),
         compiler_params=pltpu.CompilerParams(vmem_limit_bytes=62 << 20), name="update",
-    )(place, lax.optimization_barrier(place)[:, None], spread, master, first, second, total, params, norm_first, norm_second)
+    )(place, lax.optimization_barrier(place)[:, None], spread, master, first, second, total, params, norm_first, norm_second, *passed)
 
 
 def place_kernel(place_s, master, out, wide, staged, sem):
@@ -1529,8 +1541,9 @@
     spread_out, norm_total, decoded, dx0 = return_grads([*fwd[:4], *kept[3:]], norms, decoded.reshape(2, 128, DD), dx0.reshape(2, 128, DE), table,
                                                         SHARD_UNITS, GROUPS, PLAN_BACK, 2)
     norm_params = jnp.concatenate([norm_gains, norm_biases], axis=0)
-    new_master, new_first, new_second, new_norms, norm_one_new, norm_two_new = update(
-        place, spread_out.reshape(16 * SHARD_UNITS, 512), master, first_moment, second_moment, norm_total, norm_params, norm_first, norm_second)
+    new_master, new_first, new_second, new_norms, norm_one_new, norm_two_new, decoded, dx0 = update(
+        place, spread_out.reshape(16 * SHARD_UNITS, 512), master, first_moment, second_moment, norm_total, norm_params, norm_first, norm_second,
+        (decoded, dx0))
     return (decoded, dx0, new_master, new_first, new_second, new_norms, norm_one_new, norm_two_new)
 
 

time: 347 us -> 373 us (1.075)
  Pallas kernels: 331 us -> 359 us
    pallas_call x1, Pallas kernels: 14 us -> 48.4 us  [update(): pl.pallas_call(update_kernel, out_shape=out, grid_spec=pltpu.PrefetchScal...]
    pallas_call x1, Pallas kernels: 140 us -> 135 us  [spread_weights(): pl.pallas_call(partial(weights_kernel, table, groups, plan), out_shape=[S...]
where the time goes in v1:
time: 373 us; the launch traced here: 367 us
  Pallas kernels  359 us (96%)
    pallas_call x1, Pallas kernels, spread_weights(): pl.pallas_call(partial(weights_kernel, table, groups, plan), out_shape=[S...  135 us
    pallas_call x1, Pallas kernels, return_grads(): pl.pallas_call(partial(return_kernel, table, groups, plan), out_shape=(S(...  133 us
    pallas_call x1, Pallas kernels, update(): pl.pallas_call(update_kernel, out_shape=out, grid_spec=pltpu.PrefetchScal...  48.4 us
    pallas_call x1, Pallas kernels, chain(): pl.pallas_call(partial(chain_kernel, table), out_shape=outs, in_specs=[vm...  30.7 us
    pallas_call x1, Pallas kernels, place_blocks(): pl.pallas_call(place_kernel, out_shape=jax.ShapeDtypeStruct((rows, 512),...  13.3 us

profile of v1, /device:TPU:1, one launch (start us, length us, event | category | flops | bytes accessed | tf_op | source)
XLA Modules:
  0.0 367.3 jit_solution(7549658326849564828)
XLA Ops:
  0.6 0.9 compare_reduce_fusion
  1.5 0.1 fusion.3
  1.7 0.2 fusion.4
  1.9 0.1 select_reduce_fusion.1
  2.0 0.1 convert_reduce_fusion
  2.2 0.2 select_reduce_fusion
  2.3 0.7 fusion.1
  3.0 0.6 slice.7
  3.6 1.3 fusion.11.place_s
  4.9 0.0 copy-start.3
  4.9 13.3 %place_blocks.1 = bf16[10496,512]{1,0:T(8,128)(2,1)} custom-call(s32[1296]{0:T(1024)} %fusion.11.place_s, f32[1296,512]{1,0:T(8,128)} %master.3), custom_call_target="tpu_custom_call" | custom-call | tf_op jit(solution)/shard_map/place_blocks/pallas_call | solution.py:1519
  18.3 0.0 copy-done.3
  18.3 0.6 copy.28
  18.9 134.5 %spread_weights.1 = (bf16[2,4,2,2,2640,128]{5,4,3,2,1,0:T(8,128)(2,1)}, s32[2,3,128]{2,1,0:T(4,128)}, f32[2,128,512]{2,1,0:T(8,128)}, f32[256,768]{1,0:T(8,128)}...) custom-call(bf16[4,2,2,656,512]{4,3,2,1,0:T(8,128)(2,1)} %bitcast.13, ...), custom_call_target="tpu_custom_call" | custom-call | tf_op jit(solution)/shard_map/spread_weights/pallas_call | solution.py:1285
  153.4 30.7 %chain.1 = (f32[256,512]{1,0:T(8,128)}, f32[256,768]{1,0:T(8,128)}, f32[4,1280]{1,0:T(4,128)}, bf16[256,768]{1,0:T(8,128)(2,1)}, bf16[256,512]{1,0:T(8,128)(2,1)...) custom-call(s32[2,3,128]{2,1,0:T(4,128)} %get-tuple-element.57.pos, ...), custom_call_target="tpu_custom_call" | custom-call | flops 8000000000 | bytes 40000000 | tf_op jit(solution)/shard_map/chain/pallas_call | solution.py:931
  184.1 0.0 copy-start
  184.1 0.0 copy-start.1
  184.2 0.0 copy-start.2
  184.2 132.5 %return_grads.1 = (bf16[4,2,2,656,512]{4,3,2,1,0:T(8,128)(2,1)}, f32[4,1280]{1,0:T(4,128)}, f32[2,128,512]{2,1,0:T(8,128)}, f32[2,128,768]{2,1,0:T(8,128)}) custom-call(bf16[256,768]{1,0:T(8,128)(2,1)} %get-tuple-element.53.refs_0_, bf16[256,768]{1,0:T(8,128)(2,1)} %get-tuple-element.54.refs_1_, bf16[256,768]{1,0:T(8,128)(2,1)} %get-tuple-element.55.refs_2_, ...), custom_call_target="tpu_custom_call" | custom-call | tf_op jit(solution)/shard_map/return_grads/pallas_call | solution.py:1421
  316.7 0.0 copy-done
  316.7 1.1 broadcast_in_dim.48.place
  317.8 0.0 copy-done.1
  317.8 0.0 copy-done.2
  317.8 0.6 pad_maximum_fusion.params
  318.4 48.4 %update.1 = (f32[1296,512]{1,0:T(8,128)}, f32[1296,512]{1,0:T(8,128)}, f32[1296,512]{1,0:T(8,128)}, f32[4,1280]{1,0:T(4,128)}, f32[4,1280]{1,0:T(4,128)}, /*inde...) custom-call(s32[1296]{0:T(1024)} %fusion.11.place_s, s32[1296,1]{1,0:T(8,128)} %broadcast_in_dim.48.place, ...), custom_call_target="tpu_custom_call" | custom-call | tf_op jit(solution)/shard_map/update/pallas_call | solution.py:1474
  (2 shorter events, 0.0 us)
Async XLA Ops:
  4.9 13.3 %copy-start.3 = (s32[3,2,128]{2,1,0:T(2,128)S(1)}, s32[3,2,128]{2,1,0:T(2,128)}, u32[]{:S(2)}) copy-start(s32[3,2,128]{2,1,0:T(2,128)} %param.15) | copy-start | bytes 9220
  184.1 132.6 %copy-start = (s32[1296]{0:T(1024)S(1)}, s32[1296]{0:T(1024)}, u32[]{:S(2)}) copy-start(s32[1296]{0:T(1024)} %fusion.11.place_s) | copy-start | bytes 15556
  184.1 133.7 %copy-start.1 = (f32[2,1280]{1,0:T(2,128)S(1)}, f32[2,1280]{1,0:T(2,128)}, u32[]{:S(2)}) copy-start(f32[2,1280]{1,0:T(2,128)} %gains.3) | copy-start | bytes 30724
  184.2 133.6 %copy-start.2 = (f32[2,1280]{1,0:T(2,128)S(1)}, f32[2,1280]{1,0:T(2,128)}, u32[]{:S(2)}) copy-start(f32[2,1280]{1,0:T(2,128)} %biases.3) | copy-start | bytes 30724

commit v2 on v1

--- a/solution.py
+++ b/solution.py
@@ -1190,7 +1190,6 @@
 
     def start(self):
         self.w.send(self.k, self.src.at[self.give], self.out.at[self.p.x], "x")
-        self.local().start()
 
     def finish(self):
         self.w.land(self.k, self.out.at[1 - self.p.x])
@@ -1210,6 +1209,7 @@
     swaps = [Swap(p, w, a, b, 1 - p.x, p.x) for a, b in ((tok_in, tok), (pos_in, pos), (cot_in, cot))]
     for s in swaps:
         s.start()
+        s.local().start()
     lists, finishes = [], []
     for g, mats in enumerate(groups):
         u0, un, r0, rn = group_span(table, mats)
@@ -1314,6 +1314,8 @@
     p.greet(["c", "y", "x"])
     w = Wires(p, sem)
     swaps = [Swap(p, w, a, b, 1 - p.x, p.x) for a, b in ((dec_in, dec), (dx_in, dx))]
+    for s in swaps:
+        s.local().start()
     swaps[0].start()
     lists, finishes = [], []
     for g, mats in enumerate(groups):
@@ -1435,12 +1437,11 @@
     passed, refs = refs[:2], refs[2:]
     new_master, new_first, new_second, new_norms, new_nf, new_ns = refs[:6]
     i = pl.program_id(0)
-    copies = [pltpu.make_async_copy(a, b, refs[8].at[k]) for k, (a, b) in enumerate(zip(passed, refs[6:8]))]
 
     @pl.when(i == 0)
     def _():
-        for c in copies:
-            c.start()
+        for a, b in zip(passed, refs[6:8]):
+            b[...] = a[...]
         new_norms[...], new_nf[...], new_ns[...] = adamw(params[...], total[...], norm_first[...], norm_second[...], 0.0, NORM_RATE)
 
     lane = lax.broadcasted_iota(jnp.int32, (16, 256), 1)
@@ -1457,11 +1458,6 @@
         new_master[here, :], new_first[here, :], new_second[here, :] = adamw(
             master[here, :], grad, first[here, :], second[here, :], WEIGHT_DECAY, LEARN_RATE)
 
-    @pl.when(i == pl.num_programs(0) - 1)
-    def _():
-        for c in copies:
-            c.wait()
-
 
 def update(place, spread, master, first, second, total, params, norm_first, norm_second, passed):
     slots = master.shape[0]
@@ -1470,13 +1466,13 @@
     whole = lambda v: pl.BlockSpec(v.shape, lambda i, s: (0, 0), pipeline_mode=pl.Buffered(1))
     small = pl.BlockSpec(params.shape, lambda i, s: (0, 0))
     out = [S(master.shape, jnp.float32)] * 3 + [S(params.shape, jnp.float32)] * 3 + [S(v.shape, v.dtype) for v in passed]
-    hbm = pl.BlockSpec(memory_space=pl.ANY)
+    both = [pl.BlockSpec(v.shape, lambda i, s: (0, 0, 0), pipeline_mode=pl.Buffered(1)) for v in passed]
     return pl.pallas_call(
         update_kernel, out_shape=out,
         grid_spec=pltpu.PrefetchScalarGridSpec(
             num_scalar_prefetch=1, grid=(slots // STEP_ROWS,),
-            in_specs=[pl.BlockSpec((STEP_ROWS, 1), lambda i, s: (i, 0)), whole(spread), rows, rows, rows, small, small, small, small, hbm, hbm],
-            out_specs=[rows] * 3 + [small] * 3 + [hbm, hbm], scratch_shapes=[pltpu.SemaphoreType.DMA((2,))]),
+            in_specs=[pl.BlockSpec((STEP_ROWS, 1), lambda i, s: (i, 0)), whole(spread), rows, rows, rows, small, small, small, small] + both,
+            out_specs=[rows] * 3 + [small] * 3 + both),
         compiler_params=pltpu.CompilerParams(vmem_limit_bytes=62 << 20), name="update",
     )(place, lax.optimization_barrier(place)[:, None], spread, master, first, second, total, params, norm_first, norm_second, *passed)
 

time: 373 us -> 339 us (0.909)
  Pallas kernels: 359 us -> 326 us
    pallas_call x1, Pallas kernels: 48.4 us -> 14.6 us  [update(): pl.pallas_call(update_kernel, out_shape=out, grid_spec=pltpu.PrefetchScal...]
where the time goes in v2:
time: 339 us; the launch traced here: 334 us
  Pallas kernels  326 us (96%)
  other arithmetic  3.46 us (1%)
    pallas_call x1, Pallas kernels, spread_weights(): pl.pallas_call(partial(weights_kernel, table, groups, plan), out_shape=[S...  135 us
    pallas_call x1, Pallas kernels, return_grads(): pl.pallas_call(partial(return_kernel, table, groups, plan), out_shape=(S(...  133 us
    pallas_call x1, Pallas kernels, chain(): pl.pallas_call(partial(chain_kernel, table), out_shape=outs, in_specs=[vm...  30.7 us
    pallas_call x1, Pallas kernels, update(): pl.pallas_call(update_kernel, out_shape=out, grid_spec=pltpu.PrefetchScal...  14.6 us
    pallas_call x1, Pallas kernels, place_blocks(): pl.pallas_call(place_kernel, out_shape=jax.ShapeDtypeStruct((rows, 512),...  13.3 us

profile of v2, /device:TPU:1, one launch (start us, length us, event | category | flops | bytes accessed | tf_op | source)
XLA Modules:
  0.0 333.5 jit_solution(12172688528528811472)
XLA Ops:
  0.6 0.9 compare_reduce_fusion
  1.5 0.1 fusion.3
  1.7 0.2 fusion.4
  1.9 0.1 select_reduce_fusion.1
  2.0 0.1 convert_reduce_fusion
  2.2 0.2 select_reduce_fusion
  2.3 0.7 fusion.1
  3.0 0.6 slice.7
  3.6 1.3 fusion.11.place_s
  4.9 0.0 copy-start.3
  4.9 13.3 %place_blocks.1 = bf16[10496,512]{1,0:T(8,128)(2,1)} custom-call(s32[1296]{0:T(1024)} %fusion.11.place_s, f32[1296,512]{1,0:T(8,128)} %master.3), custom_call_target="tpu_custom_call" | custom-call | tf_op jit(solution)/shard_map/place_blocks/pallas_call | solution.py:1515
  18.3 0.0 copy-done.3
  18.3 0.6 copy.28
  18.9 134.5 %spread_weights.1 = (bf16[2,4,2,2,2640,128]{5,4,3,2,1,0:T(8,128)(2,1)}, s32[2,3,128]{2,1,0:T(4,128)}, f32[2,128,512]{2,1,0:T(8,128)}, f32[256,768]{1,0:T(8,128)}...) custom-call(bf16[4,2,2,656,512]{4,3,2,1,0:T(8,128)(2,1)} %bitcast.13, ...), custom_call_target="tpu_custom_call" | custom-call | tf_op jit(solution)/shard_map/spread_weights/pallas_call | solution.py:1285
  153.4 30.7 %chain.1 = (f32[256,512]{1,0:T(8,128)}, f32[256,768]{1,0:T(8,128)}, f32[4,1280]{1,0:T(4,128)}, bf16[256,768]{1,0:T(8,128)(2,1)}, bf16[256,512]{1,0:T(8,128)(2,1)...) custom-call(s32[2,3,128]{2,1,0:T(4,128)} %get-tuple-element.57.pos, ...), custom_call_target="tpu_custom_call" | custom-call | flops 8000000000 | bytes 40000000 | tf_op jit(solution)/shard_map/chain/pallas_call | solution.py:931
  184.1 0.0 copy-start
  184.1 0.0 copy-start.1
  184.2 0.0 copy-start.2
  184.2 132.6 %return_grads.1 = (bf16[4,2,2,656,512]{4,3,2,1,0:T(8,128)(2,1)}, f32[4,1280]{1,0:T(4,128)}, f32[2,128,512]{2,1,0:T(8,128)}, f32[2,128,768]{2,1,0:T(8,128)}) custom-call(bf16[256,768]{1,0:T(8,128)(2,1)} %get-tuple-element.53.refs_0_, bf16[256,768]{1,0:T(8,128)(2,1)} %get-tuple-element.54.refs_1_, bf16[256,768]{1,0:T(8,128)(2,1)} %get-tuple-element.55.refs_2_, ...), custom_call_target="tpu_custom_call" | custom-call | tf_op jit(solution)/shard_map/return_grads/pallas_call | solution.py:1423
  316.8 0.0 copy-done
  316.8 1.1 broadcast_in_dim.48.place
  317.9 0.0 copy-done.1
  317.9 0.0 copy-done.2
  317.9 0.6 pad_maximum_fusion.params
  318.5 14.6 %update.1 = (f32[1296,512]{1,0:T(8,128)}, f32[1296,512]{1,0:T(8,128)}, f32[1296,512]{1,0:T(8,128)}, f32[4,1280]{1,0:T(4,128)}, f32[4,1280]{1,0:T(4,128)}, /*inde...) custom-call(s32[1296]{0:T(1024)} %fusion.11.place_s, s32[1296,1]{1,0:T(8,128)} %broadcast_in_dim.48.place, ...), custom_call_target="tpu_custom_call" | custom-call | tf_op jit(solution)/shard_map/update/pallas_call | solution.py:1470
  (2 shorter events, 0.0 us)
Async XLA Ops:
  4.9 13.3 %copy-start.3 = (s32[3,2,128]{2,1,0:T(2,128)S(1)}, s32[3,2,128]{2,1,0:T(2,128)}, u32[]{:S(2)}) copy-start(s32[3,2,128]{2,1,0:T(2,128)} %param.15) | copy-start | bytes 9220
  184.1 132.7 %copy-start = (s32[1296]{0:T(1024)S(1)}, s32[1296]{0:T(1024)}, u32[]{:S(2)}) copy-start(s32[1296]{0:T(1024)} %fusion.11.place_s) | copy-start | bytes 15556
  184.1 133.7 %copy-start.1 = (f32[2,1280]{1,0:T(2,128)S(1)}, f32[2,1280]{1,0:T(2,128)}, u32[]{:S(2)}) copy-start(f32[2,1280]{1,0:T(2,128)} %gains.3) | copy-start | bytes 30724
  184.2 133.7 %copy-start.2 = (f32[2,1280]{1,0:T(2,128)S(1)}, f32[2,1280]{1,0:T(2,128)}, u32[]{:S(2)}) copy-start(f32[2,1280]{1,0:T(2,128)} %biases.3) | copy-start | bytes 30724

commit v3 on v2

--- a/solution.py
+++ b/solution.py
@@ -698,7 +698,7 @@
     lane = lax.broadcasted_iota(jnp.int32, (256, 128), 1)
     masks = [lane // b.size == i for i in range(b.per)]
 
-    def heads(i, _):
+    def heads(i):
         t, j = i // np_, i % np_
         q = proj[:, lanes(t * gq + j)]
         k = proj[:, lanes(t * gq + np_ + j)]
@@ -711,11 +711,10 @@
             p[i * b.per + h] = s
             total = total + dot(s.astype(jnp.bfloat16), jnp.where(masks[h], v, 0))
         att[:, lanes(i)] = total.astype(jnp.bfloat16)
-        return 0
-
-    lax.fori_loop(0, np_, heads, 0)
+
+    repeat(np_, 3, heads)
     yield
-    lax.fori_loop(np_, 2 * np_, heads, 0)
+    repeat(np_, 3, lambda i: heads(np_ + i))
     keep(1)
     yield
     need(1)
@@ -793,7 +792,7 @@
     masks = [lane // b.size == i for i in range(b.per)]
     scale = b.size ** (-0.5)
 
-    def heads(i, _):
+    def heads(i):
         t, j = i // np_, i % np_
         q = proj[:, lanes(t * gq + j)]
         k = proj[:, lanes(t * gq + np_ + j)]
@@ -814,9 +813,8 @@
         dp_out[:, lanes(t * gq + j)] = (dq * scale).astype(jnp.bfloat16)
         dp_out[:, lanes(t * gq + np_ + j)] = (dk * scale).astype(jnp.bfloat16)
         dp_out[:, lanes(t * gq + 2 * np_ + j)] = dv.astype(jnp.bfloat16)
-        return 0
-
-    lax.fori_loop(0, 2 * np_, heads, 0)
+
+    repeat(2 * np_, 2, heads)
     keep(0)
     pull(acc, dp_out, w, b.q, 9)
     dx, dg, db = ln_back(acc[...], m1[...], i1[:, :1], gains[0:1, cols])
@@ -1433,7 +1431,7 @@
 STEP_ROWS = 432
 
 
-def update_kernel(place_s, place, spread, master, first, second, total, params, norm_first, norm_second, *refs):
+def update_kernel(place, spread, master, first, second, total, params, norm_first, norm_second, *refs):
     passed, refs = refs[:2], refs[2:]
     new_master, new_first, new_second, new_norms, new_nf, new_ns = refs[:6]
     i = pl.program_id(0)
@@ -1444,17 +1442,18 @@
             b[...] = a[...]
         new_norms[...], new_nf[...], new_ns[...] = adamw(params[...], total[...], norm_first[...], norm_second[...], 0.0, NORM_RATE)
 
-    lane = lax.broadcasted_iota(jnp.int32, (16, 256), 1)
-    row = lax.broadcasted_iota(jnp.int32, (16, 256), 0)
+    lane = lax.broadcasted_iota(jnp.int32, (16, 128), 1)
+    row = lax.broadcasted_iota(jnp.int32, (16, 128), 0)
     for k in range(STEP_ROWS // 16):
-        tiles = []
+        tiles, spot = [], jnp.full((16, 128), -1, jnp.int32)
         for j in range(16):
-            at = jnp.minimum(place_s[i * STEP_ROWS + 16 * k + j] >> 4, spread.shape[0] // 16 - 1)
-            tiles.append(spread[pl.ds(pl.multiple_of(at * 16, 16), 16), :])
+            at = place[i * STEP_ROWS + 16 * k + j]
+            tile = jnp.minimum(at >> 4, spread.shape[0] // 16 - 1)
+            tiles.append(spread[pl.ds(pl.multiple_of(tile * 16, 16), 16), :])
+            spot = jnp.where(row == j, jnp.where(at < spread.shape[0], 16 * j + (at & 15), -1), spot)
         here = slice(16 * k, 16 * k + 16)
-        spot = place[here, :]
-        used = jnp.logical_and(lane == row * 16 + (spot & 15), spot < spread.shape[0])
-        grad = dot(jnp.where(used, 1.0, 0.0).astype(jnp.bfloat16), jnp.concatenate(tiles, axis=0))
+        pick = jnp.concatenate([jnp.where(lane == spot, 1.0, 0.0), jnp.where(lane + 128 == spot, 1.0, 0.0)], axis=1)
+        grad = dot(pick.astype(jnp.bfloat16), jnp.concatenate(tiles, axis=0))
         new_master[here, :], new_first[here, :], new_second[here, :] = adamw(
             master[here, :], grad, first[here, :], second[here, :], WEIGHT_DECAY, LEARN_RATE)
 
@@ -1471,10 +1470,10 @@
         update_kernel, out_shape=out,
         grid_spec=pltpu.PrefetchScalarGridSpec(
             num_scalar_prefetch=1, grid=(slots // STEP_ROWS,),
-            in_specs=[pl.BlockSpec((STEP_ROWS, 1), lambda i, s: (i, 0)), whole(spread), rows, rows, rows, small, small, small, small] + both,
+            in_specs=[whole(spread), rows, rows, rows, small, small, small, small] + both,
             out_specs=[rows] * 3 + [small] * 3 + both),
         compiler_params=pltpu.CompilerParams(vmem_limit_bytes=62 << 20), name="update",
-    )(place, lax.optimization_barrier(place)[:, None], spread, master, first, second, total, params, norm_first, norm_second, *passed)
+    )(place, spread, master, first, second, total, params, norm_first, norm_second, *passed)
 
 
 def place_kernel(place_s, master, out, wide, staged, sem):

time: 339 us -> 336 us (level)
  no operation moved by 1% of the time
where the time goes in v3:
time: 336 us; the launch traced here: 331 us
  Pallas kernels  324 us (96%)
  other arithmetic  3.45 us (1%)
    pallas_call x1, Pallas kernels, spread_weights(): pl.pallas_call(partial(weights_kernel, table, groups, plan), out_shape=[S...  134 us
    pallas_call x1, Pallas kernels, return_grads(): pl.pallas_call(partial(return_kernel, table, groups, plan), out_shape=(S(...  133 us
    pallas_call x1, Pallas kernels, chain(): pl.pallas_call(partial(chain_kernel, table), out_shape=outs, in_specs=[vm...  29.3 us
    pallas_call x1, Pallas kernels, update(): pl.pallas_call(update_kernel, out_shape=out, grid_spec=pltpu.PrefetchScal...  14.2 us
    pallas_call x1, Pallas kernels, place_blocks(): pl.pallas_call(place_kernel, out_shape=jax.ShapeDtypeStruct((rows, 512),...  13.3 us

profile of v3, /device:TPU:1, one launch (start us, length us, event | category | flops | bytes accessed | tf_op | source)
XLA Modules:
  0.0 330.8 jit_solution(10010018203533104071)
XLA Ops:
  0.6 0.9 compare_reduce_fusion
  1.5 0.1 fusion.3
  1.7 0.2 fusion.4
  1.9 0.1 select_reduce_fusion.1
  2.0 0.1 convert_reduce_fusion
  2.2 0.2 select_reduce_fusion
  2.3 0.7 fusion.1
  3.0 0.6 slice.7
  3.6 1.3 fusion.11.place_s.place
  4.9 0.0 copy-start.2
  4.9 13.3 %place_blocks.1 = bf16[10496,512]{1,0:T(8,128)(2,1)} custom-call(s32[1296]{0:T(1024)} %fusion.11.place_s.place, f32[1296,512]{1,0:T(8,128)} %master.3), custom_call_target="tpu_custom_call" | custom-call | tf_op jit(solution)/shard_map/place_blocks/pallas_call | solution.py:1514
  18.3 0.0 copy-done.2
  18.3 0.6 copy.26
  18.9 134.4 %spread_weights.1 = (bf16[2,4,2,2,2640,128]{5,4,3,2,1,0:T(8,128)(2,1)}, s32[2,3,128]{2,1,0:T(4,128)}, f32[2,128,512]{2,1,0:T(8,128)}, f32[256,768]{1,0:T(8,128)}...) custom-call(bf16[4,2,2,656,512]{4,3,2,1,0:T(8,128)(2,1)} %bitcast.13, ...), custom_call_target="tpu_custom_call" | custom-call | tf_op jit(solution)/shard_map/spread_weights/pallas_call | solution.py:1283
  153.2 29.3 %chain.1 = (f32[256,512]{1,0:T(8,128)}, f32[256,768]{1,0:T(8,128)}, f32[4,1280]{1,0:T(4,128)}, bf16[256,768]{1,0:T(8,128)(2,1)}, bf16[256,512]{1,0:T(8,128)(2,1)...) custom-call(s32[2,3,128]{2,1,0:T(4,128)} %get-tuple-element.57.pos, ...), custom_call_target="tpu_custom_call" | custom-call | flops 8000000000 | bytes 40000000 | tf_op jit(solution)/shard_map/chain/pallas_call | solution.py:929
  182.5 0.0 copy-start
  182.5 0.0 copy-start.1
  182.6 133.2 %return_grads.1 = (bf16[4,2,2,656,512]{4,3,2,1,0:T(8,128)(2,1)}, f32[4,1280]{1,0:T(4,128)}, f32[2,128,512]{2,1,0:T(8,128)}, f32[2,128,768]{2,1,0:T(8,128)}) custom-call(bf16[256,768]{1,0:T(8,128)(2,1)} %get-tuple-element.53.refs_0_, bf16[256,768]{1,0:T(8,128)(2,1)} %get-tuple-element.54.refs_1_, bf16[256,768]{1,0:T(8,128)(2,1)} %get-tuple-element.55.refs_2_, ...), custom_call_target="tpu_custom_call" | custom-call | tf_op jit(solution)/shard_map/return_grads/pallas_call | solution.py:1421
  315.8 0.0 copy-done
  315.8 0.0 copy-done.1
  315.8 0.6 pad_maximum_fusion.params
  316.4 14.2 %update.1 = (f32[1296,512]{1,0:T(8,128)}, f32[1296,512]{1,0:T(8,128)}, f32[1296,512]{1,0:T(8,128)}, f32[4,1280]{1,0:T(4,128)}, f32[4,1280]{1,0:T(4,128)}, /*inde...) custom-call(s32[1296]{0:T(1024)} %fusion.11.place_s.place, bf16[10496,512]{1,0:T(8,128)(2,1)} %bitcast.15, ...), custom_call_target="tpu_custom_call" | custom-call | tf_op jit(solution)/shard_map/update/pallas_call | solution.py:1469
  (2 shorter events, 0.0 us)
Async XLA Ops:
  4.9 13.3 %copy-start.2 = (s32[3,2,128]{2,1,0:T(2,128)S(1)}, s32[3,2,128]{2,1,0:T(2,128)}, u32[]{:S(2)}) copy-start(s32[3,2,128]{2,1,0:T(2,128)} %param.15) | copy-start | bytes 9220
  182.5 133.3 %copy-start = (f32[2,1280]{1,0:T(2,128)S(1)}, f32[2,1280]{1,0:T(2,128)}, u32[]{:S(2)}) copy-start(f32[2,1280]{1,0:T(2,128)} %gains.3) | copy-start | bytes 30724
  182.5 133.3 %copy-start.1 = (f32[2,1280]{1,0:T(2,128)S(1)}, f32[2,1280]{1,0:T(2,128)}, u32[]{:S(2)}) copy-start(f32[2,1280]{1,0:T(2,128)} %biases.3) | copy-start | bytes 30724

commit v4 on v3

--- a/solution.py
+++ b/solution.py
@@ -532,10 +532,9 @@
             unit_at = -(-unit_at // 16) * 16
         rb, panels = rows // shards, cols // PANEL
         units = rb * cols // 512
-        padded = -(-rb // 16) * 16
-        table.append((rb, panels, units, unit_at, row_at, padded, flat_at))
+        table.append((rb, panels, units, unit_at, row_at, rb, flat_at))
         unit_at += units
-        row_at += padded * panels
+        row_at += rb * panels
         flat_at += units * shards
     return table, unit_at, row_at
 
@@ -630,12 +629,12 @@
 
 
 def panel(w, t, mat, g, lo=0, num=16):
-    rb, _, _, _, at, padded, _ = mat
-    rows = pl.ds(pl.multiple_of(at + g * padded, 16), padded)
+    rb, _, _, _, at, _, _ = mat
+    if rb % 16:
+        v = w[t, lo:lo + num, at + g // 2 * 2 * rb:at + (g // 2 + 1) * 2 * rb, :].astype(jnp.float32)
+        return v[:, g % 2 * rb:(g % 2 + 1) * rb].reshape(num * rb, 128).astype(jnp.bfloat16)
+    rows = pl.ds(pl.multiple_of(at + g * rb, 16), rb)
     v = w[t, lo:lo + num, rows, :] if isinstance(lo, int) else w[t, pl.ds(lo, num), rows, :]
-    if padded > rb:
-        v = v.astype(jnp.float32)[:, :rb].reshape(num * rb, 128).astype(jnp.bfloat16)
-        return v
     return v.reshape(num * rb, 128)
 
 
@@ -944,12 +943,7 @@
     repeat(count // 128, 6, turn)
 
     def place(t, g, v):
-        if padded > rb:
-            v = v.reshape(16, rb, 128)
-            v = jnp.concatenate([v, jnp.zeros((16, padded - rb, 128), jnp.float32)], axis=1).astype(jnp.bfloat16)
-        else:
-            v = v.astype(jnp.bfloat16).reshape(16, rb, 128)
-        put(t, g, v)
+        put(t, g, v.astype(jnp.bfloat16).reshape(16, rb, 128))
 
     if m in BY_ROWS:
         half = count // 2
@@ -957,6 +951,10 @@
         def body(i):
             t, g = i // (panels // 2), i % (panels // 2)
             v = dot(turned[pl.ds(pl.multiple_of(t * half, 128), half), :], grad[:, lanes(g, 256)])
+            if rb % 16:
+                v = jnp.concatenate([v[:, :128].reshape(16, rb, 128), v[:, 128:].reshape(16, rb, 128)], axis=1)
+                put(t, 2 * g, v.astype(jnp.bfloat16))
+                return
             place(t, 2 * g, v[:, :128])
             place(t, 2 * g + 1, v[:, 128:])
 
@@ -1109,11 +1107,10 @@
         flat[pl.ds(k, count, stride=4), :] = units[:, 128 * k:128 * (k + 1)].astype(jnp.float32)
     for m in mats:
         rb, panels, n, first, _, padded, _ = table[m]
-        for g in range(panels):
-            v = flat[pl.ds(4 * (first - base) + g, rb, stride=panels), :]
-            if padded > rb:
-                v = jnp.concatenate([v, jnp.zeros((padded - rb, 128), jnp.float32)], axis=0)
-            put(m, g, v.astype(jnp.bfloat16))
+        n = 2 if rb % 16 else 1
+        for g in range(0, panels, n):
+            v = [flat[pl.ds(4 * (first - base) + g + k, rb, stride=panels), :] for k in range(n)]
+            put(m, g, jnp.concatenate(v, axis=0).astype(jnp.bfloat16))
 
 
 def panels_to_units(table, mats, take, flat, units):
@@ -1121,8 +1118,11 @@
     used = 0
     for m in mats:
         rb, panels, n, first, _, padded, _ = table[m]
-        for g in range(panels):
-            flat[pl.ds(4 * (first - base) + g, rb, stride=panels), :] = take(m, g)[:rb]
+        many = 2 if rb % 16 else 1
+        for g in range(0, panels, many):
+            v = take(m, g, many)
+            for k in range(many):
+                flat[pl.ds(4 * (first - base) + g + k, rb, stride=panels), :] = v[k * rb:(k + 1) * rb]
         used = 4 * (first - base + n)
     if used < 4 * count:
         flat[used:4 * count, :] = jnp.zeros((4 * count - used, 128), jnp.float32)
@@ -1230,7 +1230,7 @@
         def done(mats=mats, acc=acc, shard=shard, r0=r0):
             def put(m, i, v):
                 lo = table[m][4] - r0 + i * table[m][5]
-                shard[lo:lo + table[m][5], :] = v
+                shard[lo:lo + v.shape[0], :] = v
             units_to_panels(table, mats, acc.at[p.z, p.y], flat, put)
 
         ev, share, far = reduce_events(p, w, plan[0][g], own, other, buf, ready, done)
@@ -1330,9 +1330,9 @@
         def done(mats=mats, side=side, unit=unit, r0=r0):
             mine = side.at[p.c, p.x, p.z, p.y]
 
-            def take(m, i):
+            def take(m, i, many):
                 lo = table[m][4] - r0 + i * table[m][5]
-                return mine[lo:lo + table[m][5], :].astype(jnp.float32)
+                return mine[lo:lo + many * table[m][5], :].astype(jnp.float32)
             panels_to_units(table, mats, take, flat, unit)
 
         ev, share, far = reduce_events(p, w, plan[0][g], own, other, buf, lambda d: None, done)
@@ -1342,8 +1342,8 @@
                 lo, padded = table[m][4] - r0, table[m][5]
 
                 def put(t, i, v, lo=lo, padded=padded):
-                    v = v.reshape(4, 2, 2, padded, 128)
-                    rows = pl.ds(pl.multiple_of(lo + i * padded, 16), padded)
+                    v = v.reshape(4, 2, 2, v.shape[1], 128)
+                    rows = pl.ds(pl.multiple_of(lo + i * padded, 16), v.shape[3])
                     side[0, t, :, :, rows, :] = v[:, :, 0]
                     side[1, t, :, :, rows, :] = v[:, :, 1]
                 load(m).wait()
@@ -1431,7 +1431,7 @@
 STEP_ROWS = 432
 
 
-def update_kernel(place, spread, master, first, second, total, params, norm_first, norm_second, *refs):
+def update_kernel(place, spread, master, first, second, total, gains, biases, norm_first, norm_second, *refs):
     passed, refs = refs[:2], refs[2:]
     new_master, new_first, new_second, new_norms, new_nf, new_ns = refs[:6]
     i = pl.program_id(0)
@@ -1440,7 +1440,8 @@
     def _():
         for a, b in zip(passed, refs[6:8]):
             b[...] = a[...]
-        new_norms[...], new_nf[...], new_ns[...] = adamw(params[...], total[...], norm_first[...], norm_second[...], 0.0, NORM_RATE)
+        for v, r in ((gains, slice(0, 2)), (biases, slice(2, 4))):
+            new_norms[r, :], new_nf[r, :], new_ns[r, :] = adamw(v[...], total[r, :], norm_first[r, :], norm_second[r, :], 0.0, NORM_RATE)
 
     lane = lax.broadcasted_iota(jnp.int32, (16, 128), 1)
     row = lax.broadcasted_iota(jnp.int32, (16, 128), 0)
@@ -1458,22 +1459,23 @@
             master[here, :], grad, first[here, :], second[here, :], WEIGHT_DECAY, LEARN_RATE)
 
 
-def update(place, spread, master, first, second, total, params, norm_first, norm_second, passed):
+def update(place, spread, master, first, second, total, gains, biases, norm_first, norm_second, passed):
     slots = master.shape[0]
     S = jax.ShapeDtypeStruct
     rows = pl.BlockSpec((STEP_ROWS, 512), lambda i, s: (i, 0))
     whole = lambda v: pl.BlockSpec(v.shape, lambda i, s: (0, 0), pipeline_mode=pl.Buffered(1))
-    small = pl.BlockSpec(params.shape, lambda i, s: (0, 0))
-    out = [S(master.shape, jnp.float32)] * 3 + [S(params.shape, jnp.float32)] * 3 + [S(v.shape, v.dtype) for v in passed]
+    small = pl.BlockSpec(total.shape, lambda i, s: (0, 0))
+    pair_of = pl.BlockSpec(gains.shape, lambda i, s: (0, 0))
+    out = [S(master.shape, jnp.float32)] * 3 + [S(total.shape, jnp.float32)] * 3 + [S(v.shape, v.dtype) for v in passed]
     both = [pl.BlockSpec(v.shape, lambda i, s: (0, 0, 0), pipeline_mode=pl.Buffered(1)) for v in passed]
     return pl.pallas_call(
         update_kernel, out_shape=out,
         grid_spec=pltpu.PrefetchScalarGridSpec(
             num_scalar_prefetch=1, grid=(slots // STEP_ROWS,),
-            in_specs=[whole(spread), rows, rows, rows, small, small, small, small] + both,
+            in_specs=[whole(spread), rows, rows, rows, small, pair_of, pair_of, small, small] + both,
             out_specs=[rows] * 3 + [small] * 3 + both),
         compiler_params=pltpu.CompilerParams(vmem_limit_bytes=62 << 20), name="update",
-    )(place, spread, master, first, second, total, params, norm_first, norm_second, *passed)
+    )(place, spread, master, first, second, total, gains, biases, norm_first, norm_second, *passed)
 
 
 def place_kernel(place_s, master, out, wide, staged, sem):
@@ -1535,9 +1537,8 @@
     decoded, dx0, norms = kept[:3]
     spread_out, norm_total, decoded, dx0 = return_grads([*fwd[:4], *kept[3:]], norms, decoded.reshape(2, 128, DD), dx0.reshape(2, 128, DE), table,
                                                         SHARD_UNITS, GROUPS, PLAN_BACK, 2)
-    norm_params = jnp.concatenate([norm_gains, norm_biases], axis=0)
     new_master, new_first, new_second, new_norms, norm_one_new, norm_two_new, decoded, dx0 = update(
-        place, spread_out.reshape(16 * SHARD_UNITS, 512), master, first_moment, second_moment, norm_total, norm_params, norm_first, norm_second,
+        place, spread_out.reshape(16 * SHARD_UNITS, 512), master, first_moment, second_moment, norm_total, norm_gains, norm_biases, norm_first, norm_second,
         (decoded, dx0))
     return (decoded, dx0, new_master, new_first, new_second, new_norms, norm_one_new, norm_two_new)
 

time: 336 us -> 334 us (level)
  no operation moved by 1% of the time
where the time goes in v4:
time: 334 us; the launch traced here: 329 us
  Pallas kernels  322 us (96%)
    pallas_call x1, Pallas kernels, spread_weights(): pl.pallas_call(partial(weights_kernel, table, groups, plan), out_shape=[S...  134 us
    pallas_call x1, Pallas kernels, return_grads(): pl.pallas_call(partial(return_kernel, table, groups, plan), out_shape=(S(...  132 us
    pallas_call x1, Pallas kernels, chain(): pl.pallas_call(partial(chain_kernel, table), out_shape=outs, in_specs=[vm...  29.3 us
    pallas_call x1, Pallas kernels, update(): pl.pallas_call(update_kernel, out_shape=out, grid_spec=pltpu.PrefetchScal...  14.2 us
    pallas_call x1, Pallas kernels, place_blocks(): pl.pallas_call(place_kernel, out_shape=jax.ShapeDtypeStruct((rows, 512),...  13.2 us

profile of v4, /device:TPU:1, one launch (start us, length us, event | category | flops | bytes accessed | tf_op | source)
XLA Modules:
  0.0 328.7 jit_solution(2198675456405621481)
XLA Ops:
  0.6 1.3 copy.26
  1.9 0.9 compare_reduce_fusion
  2.8 0.1 fusion.3
  3.0 0.2 fusion.4
  3.1 0.1 select_reduce_fusion.1
  3.3 0.6 slice.7
  3.9 0.1 convert_reduce_fusion
  4.0 0.2 select_reduce_fusion
  4.2 0.7 fusion.1
  4.8 1.3 fusion.11.place_s.place
  6.2 13.2 %place_blocks.1 = bf16[10496,512]{1,0:T(8,128)(2,1)} custom-call(s32[1296]{0:T(1024)} %fusion.11.place_s.place, f32[1296,512]{1,0:T(8,128)} %master.3), custom_call_target="tpu_custom_call" | custom-call | tf_op jit(solution)/shard_map/place_blocks/pallas_call | solution.py:1516
  19.4 134.0 %spread_weights.1 = (bf16[2,4,2,2,2592,128]{5,4,3,2,1,0:T(8,128)(2,1)}, s32[2,3,128]{2,1,0:T(4,128)}, f32[2,128,512]{2,1,0:T(8,128)}, f32[256,768]{1,0:T(8,128)}...) custom-call(bf16[4,2,2,656,512]{4,3,2,1,0:T(8,128)(2,1)} %bitcast.13, ...), custom_call_target="tpu_custom_call" | custom-call | tf_op jit(solution)/shard_map/spread_weights/pallas_call | solution.py:1283
  153.4 29.3 %chain.1 = (f32[256,512]{1,0:T(8,128)}, f32[256,768]{1,0:T(8,128)}, f32[4,1280]{1,0:T(4,128)}, bf16[256,768]{1,0:T(8,128)(2,1)}, bf16[256,512]{1,0:T(8,128)(2,1)...) custom-call(s32[2,3,128]{2,1,0:T(4,128)} %get-tuple-element.57.pos, ...), custom_call_target="tpu_custom_call" | custom-call | flops 8000000000 | bytes 40000000 | tf_op jit(solution)/shard_map/chain/pallas_call | solution.py:928
  182.7 131.6 %return_grads.1 = (bf16[4,2,2,656,512]{4,3,2,1,0:T(8,128)(2,1)}, f32[4,1280]{1,0:T(4,128)}, f32[2,128,512]{2,1,0:T(8,128)}, f32[2,128,768]{2,1,0:T(8,128)}) custom-call(bf16[256,768]{1,0:T(8,128)(2,1)} %get-tuple-element.53.refs_0_, bf16[256,768]{1,0:T(8,128)(2,1)} %get-tuple-element.54.refs_1_, bf16[256,768]{1,0:T(8,128)(2,1)} %get-tuple-element.55.refs_2_, ...), custom_call_target="tpu_custom_call" | custom-call | tf_op jit(solution)/shard_map/return_grads/pallas_call | solution.py:1421
  314.3 14.2 %update.1 = (f32[1296,512]{1,0:T(8,128)}, f32[1296,512]{1,0:T(8,128)}, f32[1296,512]{1,0:T(8,128)}, f32[4,1280]{1,0:T(4,128)}, f32[4,1280]{1,0:T(4,128)}, /*inde...) custom-call(s32[1296]{0:T(1024)} %fusion.11.place_s.place, bf16[10496,512]{1,0:T(8,128)(2,1)} %bitcast.15, ...), custom_call_target="tpu_custom_call" | custom-call | tf_op jit(solution)/shard_map/update/pallas_call | solution.py:1471
  (2 shorter events, 0.0 us)

commit v5 on v4

--- a/solution.py
+++ b/solution.py
@@ -813,7 +813,7 @@
         dp_out[:, lanes(t * gq + np_ + j)] = (dk * scale).astype(jnp.bfloat16)
         dp_out[:, lanes(t * gq + 2 * np_ + j)] = dv.astype(jnp.bfloat16)
 
-    repeat(2 * np_, 2, heads)
+    repeat(2 * np_, 6, heads)
     keep(0)
     pull(acc, dp_out, w, b.q, 9)
     dx, dg, db = ln_back(acc[...], m1[...], i1[:, :1], gains[0:1, cols])
@@ -828,7 +828,7 @@
 
 def lookup(pos, tab, cols):
     row = lax.broadcasted_iota(jnp.int32, (48, 256), 0)
-    spots = [jnp.concatenate([pos[0, i:i + 1, :], pos[1, i:i + 1, :]], axis=1) for i in range(3)]
+    spots = [jnp.concatenate([pos[0, i], pos[1, i]], axis=1) for i in range(3)]
     hot = jnp.logical_or(jnp.logical_or(row == spots[0], row == spots[1] + 16), row == spots[2] + 32)
     hot = jnp.where(hot, 1.0, 0.0).astype(jnp.bfloat16)
     return sum(dot_tn(hot, tab[i, :, cols]) for i in range(3))
@@ -1204,7 +1204,8 @@
     p = Place()
     p.greet(["c", "y", "x"])
     w = Wires(p, sem)
-    swaps = [Swap(p, w, a, b, 1 - p.x, p.x) for a, b in ((tok_in, tok), (pos_in, pos), (cot_in, cot))]
+    swaps = [Swap(p, w, tok_in, tok, 1 - p.x, p.x), Swap(p, w, pos_in, pos, (ALL, 1 - p.x), (ALL, p.x)),
+             Swap(p, w, cot_in, cot, 1 - p.x, p.x)]
     for s in swaps:
         s.start()
         s.local().start()
@@ -1282,7 +1283,7 @@
     vmem = pl.BlockSpec(memory_space=pltpu.VMEM)
     return pl.pallas_call(
         partial(weights_kernel, table, groups, plan),
-        out_shape=[S((2, 4, 2, 2, rows, 128), bf16), S(pos.shape, pos.dtype), S(cot.shape, cot.dtype), S((256, DE), jnp.float32)]
+        out_shape=[S((2, 4, 2, 2, rows, 128), bf16), S((2, 3, 1, 128), pos.dtype), S(cot.shape, cot.dtype), S((256, DE), jnp.float32)]
         + [S(k, t) for k, t in fwd],
         in_specs=[hbm] * 4 + [vmem] * 4, out_specs=[hbm, vmem, hbm, vmem] + [hbm] * 12,
         scratch_shapes=scratch,
@@ -1531,7 +1532,7 @@
     unit, used = own_units(owners, lax.axis_index("dp"), master.shape[0])
     place = jnp.where(used, unit_places(unit, table, 16), 16 * SHARD_UNITS)
     parts = place_blocks(place, master, 16 * SHARD_UNITS)
-    full, pos, cot, x2, *fwd = spread_weights(parts.reshape(4, 2, 2, SHARD_UNITS, 512), tokens_in, positions.transpose(1, 0, 2),
+    full, pos, cot, x2, *fwd = spread_weights(parts.reshape(4, 2, 2, SHARD_UNITS, 512), tokens_in, positions[:, :, None],
                                               cotangent, segment_ids, norm_gains, norm_biases, table, rows, GROUPS, PLAN_OUT, 1)
     kept = chain(pos, segment_ids, norm_gains, norm_biases, cot.reshape(256, DD), full, x2, fwd[4:], table)
     decoded, dx0, norms = kept[:3]

time: 334 us -> 330 us (0.988)
  no operation moved by 1% of the time
where the time goes in v5:
time: 330 us; the launch traced here: 325 us
  Pallas kernels  320 us (97%)
    pallas_call x1, Pallas kernels, spread_weights(): pl.pallas_call(partial(weights_kernel, table, groups, plan), out_shape=[S...  134 us
    pallas_call x1, Pallas kernels, return_grads(): pl.pallas_call(partial(return_kernel, table, groups, plan), out_shape=(S(...  131 us
    pallas_call x1, Pallas kernels, chain(): pl.pallas_call(partial(chain_kernel, table), out_shape=outs, in_specs=[vm...  27.6 us
    pallas_call x1, Pallas kernels, update(): pl.pallas_call(update_kernel, out_shape=out, grid_spec=pltpu.PrefetchScal...  14.2 us
    pallas_call x1, Pallas kernels, place_blocks(): pl.pallas_call(place_kernel, out_shape=jax.ShapeDtypeStruct((rows, 512),...  13.2 us

profile of v5, /device:TPU:1, one launch (start us, length us, event | category | flops | bytes accessed | tf_op | source)
XLA Modules:
  0.0 325.4 jit_solution(13057729547825277169)
XLA Ops:
  0.6 0.9 compare_reduce_fusion
  1.5 0.1 fusion.3
  1.7 0.2 fusion.4
  1.9 0.1 select_reduce_fusion.1
  2.0 0.6 slice.7
  2.6 0.1 convert_reduce_fusion
  2.7 0.2 select_reduce_fusion
  2.9 0.7 fusion.1
  3.6 1.3 fusion.11.place_s.place
  4.9 13.2 %place_blocks.1 = bf16[10496,512]{1,0:T(8,128)(2,1)} custom-call(s32[1296]{0:T(1024)} %fusion.11.place_s.place, f32[1296,512]{1,0:T(8,128)} %master.3), custom_call_target="tpu_custom_call" | custom-call | tf_op jit(solution)/shard_map/place_blocks/pallas_call | solution.py:1517
  18.1 134.2 %spread_weights.1 = (bf16[2,4,2,2,2592,128]{5,4,3,2,1,0:T(8,128)(2,1)}, s32[2,3,1,128]{3,2,1,0:T(1,128)}, f32[2,128,512]{2,1,0:T(8,128)}, f32[256,768]{1,0:T(8,1...) custom-call(bf16[4,2,2,656,512]{4,3,2,1,0:T(8,128)(2,1)} %bitcast.11, ...), custom_call_target="tpu_custom_call" | custom-call | tf_op jit(solution)/shard_map/spread_weights/pallas_call | solution.py:1284
  152.3 27.6 %chain.1 = (f32[256,512]{1,0:T(8,128)}, f32[256,768]{1,0:T(8,128)}, f32[4,1280]{1,0:T(4,128)}, bf16[256,768]{1,0:T(8,128)(2,1)}, bf16[256,512]{1,0:T(8,128)(2,1)...) custom-call(s32[2,3,1,128]{3,2,1,0:T(1,128)} %get-tuple-element.57.p, ...), custom_call_target="tpu_custom_call" | custom-call | flops 8000000000 | bytes 40000000 | tf_op jit(solution)/shard_map/chain/pallas_call | solution.py:928
  179.9 131.0 %return_grads.1 = (bf16[4,2,2,656,512]{4,3,2,1,0:T(8,128)(2,1)}, f32[4,1280]{1,0:T(4,128)}, f32[2,128,512]{2,1,0:T(8,128)}, f32[2,128,768]{2,1,0:T(8,128)}) custom-call(bf16[256,768]{1,0:T(8,128)(2,1)} %get-tuple-element.53.refs_0_, bf16[256,768]{1,0:T(8,128)(2,1)} %get-tuple-element.54.refs_1_, bf16[256,768]{1,0:T(8,128)(2,1)} %get-tuple-element.55.refs_2_, ...), custom_call_target="tpu_custom_call" | custom-call | tf_op jit(solution)/shard_map/return_grads/pallas_call | solution.py:1422
  310.9 14.2 %update.1 = (f32[1296,512]{1,0:T(8,128)}, f32[1296,512]{1,0:T(8,128)}, f32[1296,512]{1,0:T(8,128)}, f32[4,1280]{1,0:T(4,128)}, f32[4,1280]{1,0:T(4,128)}, /*inde...) custom-call(s32[1296]{0:T(1024)} %fusion.11.place_s.place, bf16[10496,512]{1,0:T(8,128)(2,1)} %bitcast.13, ...), custom_call_target="tpu_custom_call" | custom-call | tf_op jit(solution)/shard_map/update/pallas_call | solution.py:1472
  (2 shorter events, 0.0 us)

commit v6 on v5

--- a/solution.py
+++ b/solution.py
@@ -1489,11 +1489,11 @@
     lax.fori_loop(0, count, clear, 0)
 
     def turn(i, _):
-        for j in range(16):
-            wide[pl.ds(place_s[i * 16 + j], 1), :] = master[pl.ds(i * 16 + j, 1), :]
+        for j in range(48):
+            wide[pl.ds(place_s[i * 48 + j], 1), :] = master[pl.ds(i * 48 + j, 1), :]
         return 0
 
-    lax.fori_loop(0, master.shape[0] // 16, turn, 0)
+    lax.fori_loop(0, master.shape[0] // 48, turn, 0)
     parts = 4
     part = count // parts * 64
 

time: 330 us -> 330 us (level)
  no operation moved by 1% of the time
where the time goes in v6:
time: 330 us; the launch traced here: 325 us
  Pallas kernels  320 us (97%)
    pallas_call x1, Pallas kernels, spread_weights(): pl.pallas_call(partial(weights_kernel, table, groups, plan), out_shape=[S...  134 us
    pallas_call x1, Pallas kernels, return_grads(): pl.pallas_call(partial(return_kernel, table, groups, plan), out_shape=(S(...  131 us
    pallas_call x1, Pallas kernels, chain(): pl.pallas_call(partial(chain_kernel, table), out_shape=outs, in_specs=[vm...  27.6 us
    pallas_call x1, Pallas kernels, update(): pl.pallas_call(update_kernel, out_shape=out, grid_spec=pltpu.PrefetchScal...  14.2 us
    pallas_call x1, Pallas kernels, place_blocks(): pl.pallas_call(place_kernel, out_shape=jax.ShapeDtypeStruct((rows, 512),...  13 us

profile of v6, /device:TPU:1, one launch (start us, length us, event | category | flops | bytes accessed | tf_op | source)
XLA Modules:
  0.0 325.2 jit_solution(16772779567899651301)
XLA Ops:
  0.6 0.9 compare_reduce_fusion
  1.5 0.1 fusion.3
  1.7 0.2 fusion.4
  1.9 0.1 select_reduce_fusion.1
  2.0 0.6 slice.7
  2.6 0.1 convert_reduce_fusion
  2.7 0.2 select_reduce_fusion
  2.9 0.7 fusion.1
  3.6 1.3 fusion.11.place_s.place
  4.9 13.0 %place_blocks.1 = bf16[10496,512]{1,0:T(8,128)(2,1)} custom-call(s32[1296]{0:T(1024)} %fusion.11.place_s.place, f32[1296,512]{1,0:T(8,128)} %master.3), custom_call_target="tpu_custom_call" | custom-call | tf_op jit(solution)/shard_map/place_blocks/pallas_call | solution.py:1517
  17.9 134.2 %spread_weights.1 = (bf16[2,4,2,2,2592,128]{5,4,3,2,1,0:T(8,128)(2,1)}, s32[2,3,1,128]{3,2,1,0:T(1,128)}, f32[2,128,512]{2,1,0:T(8,128)}, f32[256,768]{1,0:T(8,1...) custom-call(bf16[4,2,2,656,512]{4,3,2,1,0:T(8,128)(2,1)} %bitcast.11, ...), custom_call_target="tpu_custom_call" | custom-call | tf_op jit(solution)/shard_map/spread_weights/pallas_call | solution.py:1284
  152.1 27.6 %chain.1 = (f32[256,512]{1,0:T(8,128)}, f32[256,768]{1,0:T(8,128)}, f32[4,1280]{1,0:T(4,128)}, bf16[256,768]{1,0:T(8,128)(2,1)}, bf16[256,512]{1,0:T(8,128)(2,1)...) custom-call(s32[2,3,1,128]{3,2,1,0:T(1,128)} %get-tuple-element.57.p, ...), custom_call_target="tpu_custom_call" | custom-call | flops 8000000000 | bytes 40000000 | tf_op jit(solution)/shard_map/chain/pallas_call | solution.py:928
  179.7 131.0 %return_grads.1 = (bf16[4,2,2,656,512]{4,3,2,1,0:T(8,128)(2,1)}, f32[4,1280]{1,0:T(4,128)}, f32[2,128,512]{2,1,0:T(8,128)}, f32[2,128,768]{2,1,0:T(8,128)}) custom-call(bf16[256,768]{1,0:T(8,128)(2,1)} %get-tuple-element.53.refs_0_, bf16[256,768]{1,0:T(8,128)(2,1)} %get-tuple-element.54.refs_1_, bf16[256,768]{1,0:T(8,128)(2,1)} %get-tuple-element.55.refs_2_, ...), custom_call_target="tpu_custom_call" | custom-call | tf_op jit(solution)/shard_map/return_grads/pallas_call | solution.py:1422
  310.7 14.2 %update.1 = (f32[1296,512]{1,0:T(8,128)}, f32[1296,512]{1,0:T(8,128)}, f32[1296,512]{1,0:T(8,128)}, f32[4,1280]{1,0:T(4,128)}, f32[4,1280]{1,0:T(4,128)}, /*inde...) custom-call(s32[1296]{0:T(1024)} %fusion.11.place_s.place, bf16[10496,512]{1,0:T(8,128)(2,1)} %bitcast.13, ...), custom_call_target="tpu_custom_call" | custom-call | tf_op jit(solution)/shard_map/update/pallas_call | solution.py:1472
  (2 shorter events, 0.0 us)
